TPU v7x, 32 devices: a whole 2x2x4 slice. The times are simulated.
32 devices in a mesh: dp: 4 (over y, x), ctx: 8 (over z, core).
Axes of the slice: x: 2, y: 2, z: 4, core: 2. Of those that a mesh axis runs over, the one named last changes fastest.
Arguments:
- tokens: bfloat16 [4096, 2048], P('ctx', 'dp'), may hold values from -6 to 6
- input_gain: float32 [2048], replicated, may hold values from 0.1 to 1.9
- projections: bfloat16 [3, 2048, 1024], P(None, 'dp'), may hold values from -0.125 to 0.125
- head_gain: float32 [1024], P('dp'), may hold values from 0.1 to 1.9
Outputs:
- attended: bfloat16 [4096, 1024], P('ctx', 'dp')
All inputs are finite; a program needn't handle non-finite values.
Results may differ from a plain program's by a relative error of at most 0.0061.
Values may be sent and summed in bfloat16 or wider, within the bound.
No kernel may reach another device: no remote copies, remote signals or barrier semaphores. Data moves between devices by JAX's collectives and lax.ppermute only.
A program may use at most 64 MiB of HBM per device.

v0:
```python
import jax
import jax.numpy as jnp
from jax import lax
from jax.sharding import PartitionSpec as P

HEAD_DIM = 128


epsilon = 1e-05


def entering(value, axis, join, neutral):
    count, mine = (lax.axis_size(axis), lax.axis_index(axis))
    pieces = lax.all_gather(value, axis)
    subtotal = jnp.full_like(value, 0) + jnp.asarray(neutral, value.dtype)

    def turn(position, subtotal):
        longer = join(subtotal, pieces[position])
        return jnp.where(position < mine, longer, subtotal)

    return lax.fori_loop(0, count - 1, turn, subtotal)


def feature(inputs):
    return jnp.where(inputs > 0, inputs + 1.0, jnp.exp(jnp.minimum(inputs, 0.0)))


def activate(products):
    return jnp.concatenate([feature(products[:2]), products[2:]], axis=0).astype(jnp.bfloat16)


def combine(earlier, later):
    return earlier + later


def body(tokens, input_gain, projections, head_gain):
    whole = lax.all_gather(tokens, "dp", axis=1, tiled=True)
    inputs = whole.astype(jnp.float32)
    steps = inputs.shape[0]
    scale = lax.rsqrt(jnp.mean(inputs * inputs, axis=-1, keepdims=True) + epsilon)
    normed = (inputs * scale * input_gain).astype(jnp.bfloat16)
    width = head_gain.shape[0]
    mine = lax.all_to_all(projections, "dp", split_axis=2, concat_axis=1, tiled=True)
    products = jnp.einsum("td,pdc->ptc", normed, mine, preferred_element_type=jnp.float32)
    stacked = activate(products)
    heads = width // HEAD_DIM
    queries = stacked[0].reshape(steps, heads, HEAD_DIM)
    key_feats = stacked[1].reshape(steps, heads, HEAD_DIM)
    values = stacked[2].reshape(steps, heads, HEAD_DIM)
    local_state = jnp.einsum("the,thf->hef", key_feats, values, preferred_element_type=jnp.float32)
    prior = entering(local_state, "ctx", combine, jnp.zeros_like(local_state))
    prior_state = prior.astype(jnp.bfloat16)
    positions = jnp.arange(steps, dtype=jnp.int32)
    causal = positions[:, None] >= positions[None, :]
    scores = jnp.einsum("the,she->hts", queries, key_feats, preferred_element_type=jnp.float32)
    scores = jnp.where(causal[None], scores, 0.0).astype(jnp.bfloat16)
    inner = jnp.einsum("hts,shf->thf", scores, values, preferred_element_type=jnp.float32)
    outer = jnp.einsum("the,hef->thf", queries, prior_state, preferred_element_type=jnp.float32)
    mixed_out = inner + outer
    factor = lax.rsqrt(jnp.mean(mixed_out * mixed_out, axis=-1, keepdims=True) + epsilon)
    attended = mixed_out * factor * head_gain.reshape(heads, HEAD_DIM)
    return attended.astype(jnp.bfloat16).reshape(steps, width)


def solution(mesh):
    in_specs = (P("ctx", "dp"), P(), P(None, "dp", None), P("dp"))
    out_specs = P("ctx", "dp")
    return jax.shard_map(body, mesh=mesh, in_specs=in_specs, out_specs=out_specs, check_vma=False)
```

profile of v0, /device:TPU:0, one launch (start us, length us, event | category | flops | bytes accessed | tf_op | source)
XLA Modules:
  0.0 136.9 jit_solution(17386029378452002127)
XLA Ops:
  6.5 0.0 all-gather.4.cloned.1.call-start
  6.5 0.7 all-gather.4.cloned.1.call-update
  7.3 0.0 all-gather.6.cloned.1.call-start
  7.3 7.6 %copy.10 = bf16[3,512,1024]{1,0,2:T(4,128)(2,1)} copy(bf16[3,512,1024]{2,1,0:T(8,128)(2,1)} %param.8) | data formatting | bytes 6291456 | tf_op args[2]
  14.9 69.5 %all_to_all.18 = bf16[3,512,1024]{1,0,2:T(4,128)(2,1)S(1)} all-to-all(bf16[3,512,1024]{1,0,2:T(4,128)(2,1)} %copy.10), channel_id=1, replica_groups=mesh['dp'=4,'ctx'=8] {'dp'}, dimensions={2} | all-to-all | bytes 6291456 | tf_op jit(solution)/shard_map/all_to_all | solution.py:43
  84.4 3.0 %copy.20 = bf16[3,512,4,256]{1,2,3,0:T(4,128)(2,1)S(1)} copy(bf16[3,512,4,256]{1,0,3,2:T(4,128)(2,1)S(1)} %bitcast.32) | data formatting | bytes 6291456 | tf_op jit(solution)/shard_map/all_to_all | solution.py:43
  87.4 0.0 copy-start.1
  87.4 4.0 %all_to_all.16 = bf16[3,2048,256]{1,2,0:T(8,128)(2,1)} reshape(bf16[3,4,512,256]{2,1,3,0:T(4,128)(2,1)S(1)} %bitcast.33) | data formatting | bytes 6291456 | tf_op jit(solution)/shard_map/all_to_all | solution.py:43
  91.4 0.0 all-gather.4.cloned.1.call-done
  91.4 2.1 %fusion = f32[512]{0:T(512)S(1)} fusion(bf16[512,2048]{1,0:T(8,128)(2,1)} %all-gather.4.cloned.1.call-done), kind=kLoop, calls=%fused_computation.3 | loop fusion | flops 3145216 | bytes 2099200 | tf_op jit(solution)/shard_map/reduce_sum | solution.py:40
  93.5 0.0 copy-done.1
  93.5 4.4 %fusion.8 = f32[3,512,256]{1,2,0:T(8,128)S(1)} fusion(bf16[3,2048,256]{1,2,0:T(8,128)(2,1)} %all_to_all.16, bf16[512,2048]{1,0:T(8,128)(2,1)} %all-gather.4.cloned.1.call-done, f32[2048]{0:T(1024)S(1)} %copy-done.1, f32[512]{0:T(512)S(1)} %add_rsqrt_fusion.1), kind=kOutput, calls=%fused_computation.12 | convolution fusion | flops 1614807040 | bytes 6825984 | tf_op jit(solution)/shard_map/td,pdc->ptc/dot_general | solution.py:44
  97.9 0.2 select_convert_fusion.1
  98.2 0.9 fusion.20
  99.1 0.0 copy-start
  99.1 0.0 all-gather.6.cloned.1.call-update
  99.1 0.1 iota_compare_fusion
  99.2 22.0 %all-gather.6.cloned.1.call-done = f32[16,128,128]{2,1,0:T(8,128)} async-done(((f32[2,128,128]{2,1,0:T(8,128)}), f32[16,128,128]{2,1,0:T(8,128)}) %all-gather.6.cloned.1.call-update) | async-done | bytes 1048592 | tf_op jit(solution)/shard_map/all_gather | solution.py:14
  121.3 6.8 %while.14 = (s32[]{:T(128)}, f32[2,128,128]{2,1,0:T(8,128)S(1)}, s32[]{:T(128)}, f32[8,2,128,128]{3,2,1,0:T(8,128)}, s32[]{:T(128)}, /*index=5*/s32[]{:T(128)}) while((s32[]{:T(128)}, f32[2,128,128]{2,1,0:T(8,128)S(1)}, s32[]{:T(128)}, f32[8,2,128,128]{3,2,1,0:T(8,128)}, s32[]{:T(128)}, /*index=5*/s32[]{:T(128)}) %tuple.41), condition=%wide.region_2.3_spmd.clone, body=%wide.region_1.2_spmd.clone.sunk | while | flops 98308 | bytes 393317 | solution.py:21
  121.3 0.9 add_select_fusion.2
  122.2 0.9 add_select_fusion.2
  123.2 0.9 add_select_fusion.2
  124.2 0.9 add_select_fusion.2
  125.1 0.9 add_select_fusion.2
  126.1 0.9 add_select_fusion.2
  127.1 0.9 add_select_fusion.2
  128.1 0.3 fusion.16
  128.3 0.8 multiply_reduce_fusion
  129.1 0.0 copy-done
  129.2 0.1 multiply_convert_fusion
  129.3 0.8 copy.15
  (5 shorter events, 0.1 us)
Async XLA Ops:
  6.5 84.8 %all-gather.4.cloned.1.call-start = ((), (), s32[]{:S(2)}) async-start(), calls=%async_computation.1 | async-start | bytes 2621440 | tf_op jit(solution)/shard_map/all_gather | solution.py:37
  7.3 114.0 %all-gather.6.cloned.1.call-start = ((), (), s32[]{:S(2)}) async-start(), calls=%async_computation.2 | async-start | bytes 1179648 | tf_op jit(solution)/shard_map/all_gather | solution.py:14
  87.4 6.1 %copy-start.1 = (f32[2048]{0:T(1024)S(1)}, f32[2048]{0:T(1024)}, u32[]{:S(2)}) copy-start(f32[2048]{0:T(1024)} %param.7) | copy-start | bytes 24580
  99.1 30.0 %copy-start = (f32[256]{0:T(256)S(1)}, f32[256]{0:T(256)}, u32[]{:S(2)}) copy-start(f32[256]{0:T(256)} %param.9) | copy-start | bytes 3076
Sparse Core Ops, SparseCore 0:
  9.2 70.0 all-gather.3
  99.3 21.9 all-gather.5
where the time goes:
time: 137 us
  blocking collectives  69.5 us (51%)
  waiting for transfers between devices  22.7 us (17%)
  local copies, waits for them, and re-layouts  15.5 us (11%)
  between operations  13.5 us (10%)
  other arithmetic  9.16 us (7%)
  matrix products  6.37 us (5%)
    all_to_all x1, blocking collectives, body(): lax.all_to_all(projections, 'dp', split_axis=2, concat_axis=1, tiled=True)  69.5 us
    all_gather x1, waiting for transfers between devices, entering(): pieces = lax.all_gather(value, axis)  22 us
    unnamed x5, local copies, waits for them, and re-layouts  7.62 us
    all_to_all x2, local copies, waits for them, and re-layouts, body(): lax.all_to_all(projections, 'dp', split_axis=2, concat_axis=1, tiled=True)  6.93 us
    select_n x7, other arithmetic, turn(): return jnp.where(position < mine, longer, subtotal)  6.65 us
    dot_general x1, matrix products, body(): jnp.einsum('td,pdc->ptc', normed, mine, preferred_element_type=jnp.float32)  4.42 us
  transfers between devices with their start and end apart: 2, of which 1 were waited for; matrix products, arithmetic and copies ran while one was open for 8% of the time, Pallas kernels for 0%

commit v1 on v0

v1 whole, which is shorter than its diff:
```python
import jax
import jax.numpy as jnp
from jax import lax
from jax.experimental import pallas as pl
from jax.experimental.pallas import tpu as pltpu
from jax.sharding import PartitionSpec as P

HEAD_DIM = 128
epsilon = 1e-05
F32 = jnp.float32
BF16 = jnp.bfloat16
Q, K, V = 0, 1, 2


def feature(inputs):
    return jnp.where(inputs > 0, inputs + 1.0, jnp.exp(jnp.minimum(inputs, 0.0)))


def mm(a, b):
    return jnp.dot(a, b, preferred_element_type=F32)


def gained(x_ref, g_ref):
    return (x_ref[...].astype(F32) * g_ref[...]).astype(BF16)


def xor_pairs(size, bits):
    return [(i, i ^ bits) for i in range(size)]


def body(tokens, input_gain, projections, head_gain):
    steps, features = tokens.shape
    width = head_gain.shape[0]
    n_dp = lax.axis_size("dp")
    n_ctx = lax.axis_size("ctx")
    heads = width // HEAD_DIM
    total = features * n_dp
    assert n_dp == 4 and heads == 2 and n_ctx % 2 == 0
    H = HEAD_DIM
    mine = lax.axis_index("dp").astype(jnp.int32)
    where = jnp.full((1,), mine, jnp.int32)
    gain = input_gain.reshape(1, total)

    x_spec = pl.BlockSpec((steps, features), lambda i, m: (0, 0))
    g_spec = pl.BlockSpec((1, features), lambda i, m: (0, m[0]))

    def w_slot(matrix, bits, slot):
        return pl.BlockSpec((None, features, H), lambda i, m: (matrix, 0, (m[0] ^ bits) * 2 + slot))

    def w_both(matrix, bits):
        return pl.BlockSpec((None, features, width), lambda i, m: (matrix, 0, m[0] ^ bits))

    def cols(n, at=0):
        return pl.BlockSpec((steps, n), lambda i, m: (0, at))

    def call(kernel, name, ins, outs, flops):
        specs = [s for s, _ in ins]
        arrays = [a for _, a in ins]
        moved = sum(a.size * a.dtype.itemsize for s, a in ins if a is not projections)
        moved += sum(s.size * s.dtype.itemsize for s in outs)
        return pl.pallas_call(
            kernel,
            name=name,
            grid_spec=pltpu.PrefetchScalarGridSpec(
                num_scalar_prefetch=1,
                grid=(1,),
                in_specs=specs,
                out_specs=[pl.BlockSpec(o.shape, lambda i, m, r=len(o.shape): (0,) * r) for o in outs],
            ),
            out_shape=outs,
            cost_estimate=pl.CostEstimate(flops=flops, bytes_accessed=moved, transcendentals=0),
        )(where, *arrays)

    def arr(*shape, dtype=BF16):
        return jax.ShapeDtypeStruct(shape, dtype)

    base = [(x_spec, tokens), (g_spec, gain)]
    block = 2 * steps * features * H

    def w(spec):
        return (spec, projections)

    def first_kernel(m, x, g, w01, w03, w12, w13, o0, o1):
        xg = gained(x, g)
        o0[:, :H] = mm(xg, w01[...]).astype(BF16)
        o0[:, H:] = mm(xg, w03[...]).astype(BF16)
        o1[:, :H] = mm(xg, w12[...]).astype(BF16)
        o1[:, H:] = mm(xg, w13[...]).astype(BF16)

    def first(matrix, name):
        ins = base + [w(w_slot(matrix, 1, 0)), w(w_slot(matrix, 3, 0)), w(w_slot(matrix, 2, 1)), w(w_slot(matrix, 3, 1))]
        s0, s1 = call(first_kernel, name, ins, [arr(steps, 2 * H)] * 2, 4 * block)
        return lax.ppermute(s0, "dp", xor_pairs(n_dp, 1)), lax.ppermute(s1, "dp", xor_pairs(n_dp, 2))

    k1 = first(K, "first_k")
    v1 = first(V, "first_v")

    def squares_kernel(m, x, o):
        xf = x[...].astype(F32)
        sq = xf * xf
        hi = sq.astype(BF16)
        lo = (sq - hi.astype(F32)).astype(BF16)
        ones = jnp.ones((8, features), BF16)
        dims = (((1,), (1,)), ((), ()))
        o[...] = lax.dot_general(ones, hi, dims, preferred_element_type=F32) + lax.dot_general(ones, lo, dims, preferred_element_type=F32)

    (sq,) = call(squares_kernel, "squares", base[:1], [arr(8, steps, dtype=F32)], block // 8)
    sq_others = [lax.ppermute(sq, "dp", xor_pairs(n_dp, b)) for b in (1, 2, 3)]

    def second_kernel(m, x, g, w02, w11, r0, r1, o0, o1):
        xg = gained(x, g)
        o0[...] = (mm(xg, w02[...]) + r0[...].astype(F32)).astype(BF16)
        o1[...] = (mm(xg, w11[...]) + r1[...].astype(F32)).astype(BF16)

    def second(matrix, received, name):
        ins = base + [w(w_slot(matrix, 2, 0)), w(w_slot(matrix, 1, 1)), (cols(H, 1), received[0]), (cols(H, 1), received[1])]
        s0, s1 = call(second_kernel, name, ins, [arr(steps, H)] * 2, 2 * block)
        return lax.ppermute(s0, "dp", xor_pairs(n_dp, 2)), lax.ppermute(s1, "dp", xor_pairs(n_dp, 1))

    k2 = second(K, k1, "second_k")
    v2 = second(V, v1, "second_v")

    def query_kernel(m, x, g, w1, w2, w3, o1, o2, o3):
        xg = gained(x, g)
        for wr, o in ((w1, o1), (w2, o2), (w3, o3)):
            o[...] = mm(xg, wr[...]).astype(BF16)

    ins = base + [w(w_both(Q, b)) for b in (1, 2, 3)]
    sends = call(query_kernel, "query", ins, [arr(steps, width)] * 3, 6 * block)
    q_others = [lax.ppermute(s, "dp", xor_pairs(n_dp, b)) for b, s in zip((1, 2, 3), sends)]

    row = pl.BlockSpec((8, steps), lambda i, m: (0, 0))
    scale_spec = cols(H)

    def keys_kernel(m, x, g, wk, wv, s0, s1, s2, s3, ka0, ka1, kb0, kb1, va0, va1, o_k, o_v, o_s):
        ss = s0[...] + s1[...] + s2[...] + s3[...]
        inv = lax.rsqrt(ss * (1.0 / total) + epsilon)
        scale = jnp.broadcast_to(inv[:1, :], (H, steps)).T
        o_s[...] = scale
        xg = gained(x, g)
        own = mm(xg, wk[...])
        for h, (a, b) in enumerate(((ka0, kb0), (ka1, kb1))):
            at = slice(h * H, h * H + H)
            u = (own[:, at] + a[...].astype(F32) + b[...].astype(F32)) * scale
            o_k[:, at] = feature(u).astype(BF16)
        own = mm(xg, wv[...])
        for h, a in enumerate((va0, va1)):
            at = slice(h * H, h * H + H)
            o_v[:, at] = own[:, at] + a[...].astype(F32)

    ins = base + [w(w_both(K, 0)), w(w_both(V, 0)), (row, sq)] + [(row, s) for s in sq_others]
    ins += [(cols(H), k1[0]), (cols(H), k1[1]), (cols(H), k2[0]), (cols(H), k2[1]), (cols(H), v1[0]), (cols(H), v1[1])]
    outs = [arr(steps, width), arr(steps, width, dtype=F32), arr(steps, H, dtype=F32)]
    keys, v_own, scale = call(keys_kernel, "keys", ins, outs, 4 * block)

    def values_kernel(m, k, v, s, b0, b1, o_v, o_st):
        for h, b in enumerate((b0, b1)):
            at = slice(h * H, h * H + H)
            val = ((v[:, at] + b[...].astype(F32)) * s[...]).astype(BF16)
            o_v[:, at] = val
            o_st[h] = lax.dot_general(k[:, at], val, (((0,), (0,)), ((), ())), preferred_element_type=F32)

    ins = [(cols(width), keys), (cols(width), v_own), (scale_spec, scale), (cols(H), v2[0]), (cols(H), v2[1])]
    outs = [arr(steps, width), arr(heads, H, H, dtype=F32)]
    values, state = call(values_kernel, "values", ins, outs, 4 * steps * H * H)

    prior = entering(state, n_ctx)

    def query_act(m, x, g, wq, s, r1, r2, r3, at, xg):
        own = mm(xg, wq[:, at])
        u = own + r1[:, at].astype(F32) + r2[:, at].astype(F32) + r3[:, at].astype(F32)
        return feature(u * s[...]).astype(BF16)

    def inner_kernel(m, x, g, wq, s, r1, r2, r3, k, v, o_q, o_m):
        xg = gained(x, g)
        rows = lax.broadcasted_iota(jnp.int32, (steps, steps), 0)
        columns = lax.broadcasted_iota(jnp.int32, (steps, steps), 1)
        causal = rows >= columns
        for h in range(heads):
            at = slice(h * H, h * H + H)
            q = query_act(m, x, g, wq, s, r1, r2, r3, at, xg)
            o_q[:, at] = q
            sc = lax.dot_general(q, k[:, at], (((1,), (1,)), ((), ())), preferred_element_type=F32)
            sc = jnp.where(causal, sc, 0.0).astype(BF16)
            o_m[:, at] = mm(sc, v[:, at])

    ins = base + [w(w_both(Q, 0)), (scale_spec, scale)] + [(cols(width), r) for r in q_others] + [(cols(width), keys), (cols(width), values)]
    outs = [arr(steps, width), arr(steps, width, dtype=F32)]
    queries, inner = call(inner_kernel, "inner", ins, outs, 2 * block + 8 * steps * steps * H)

    def outer_kernel(m, q, inner, st, hg, o):
        for h in range(heads):
            at = slice(h * H, h * H + H)
            mixed = inner[:, at] + mm(q[:, at], st[h])
            factor = lax.rsqrt(jnp.mean(mixed * mixed, axis=-1, keepdims=True) + epsilon)
            o[:, at] = (mixed * factor * hg[:, at]).astype(BF16)

    st_spec = pl.BlockSpec((heads, H, H), lambda i, m: (0, 0, 0))
    hg_spec = pl.BlockSpec((1, width), lambda i, m: (0, 0))
    ins = [(cols(width), queries), (cols(width), inner), (st_spec, prior), (hg_spec, head_gain.reshape(1, width))]
    (out,) = call(outer_kernel, "outer", ins, [arr(steps, width)], 4 * steps * H * H)
    return out


def entering(state, n_ctx):
    at = lax.axis_index("ctx")
    odd = (at & 1) == 1
    own = jnp.where(odd, state[1], state[0])
    give = jnp.where(odd, state[0], state[1]).astype(BF16)
    partner = lax.ppermute(give, "ctx", xor_pairs(n_ctx, 1)).astype(F32)
    group = own + partner
    before = jnp.zeros_like(own)
    chips, span = n_ctx // 2, 1
    while span < chips:
        radix = 4 if chips % (span * 4) == 0 else 2
        digit = (at // (2 * span)) % radix
        sent = group.astype(BF16)
        for bits in range(1, radix):
            came = lax.ppermute(sent, "ctx", xor_pairs(n_ctx, 2 * span * bits)).astype(F32)
            before = before + jnp.where((digit ^ bits) < digit, came, 0.0)
            group = group + came
        span *= radix
    assert span == chips
    theirs = before + jnp.where(odd, 0.0, own)
    ours = (before + jnp.where(odd, partner, 0.0)).astype(BF16)
    other = lax.ppermute(theirs.astype(BF16), "ctx", xor_pairs(n_ctx, 1))
    return jnp.stack([jnp.where(odd, other, ours), jnp.where(odd, ours, other)])


def solution(mesh):
    in_specs = (P("ctx", "dp"), P(), P(None, "dp", None), P("dp"))
    out_specs = P("ctx", "dp")
    return jax.shard_map(body, mesh=mesh, in_specs=in_specs, out_specs=out_specs, check_vma=False)
```

time: 137 us -> 78.3 us (0.57)
  blocking collectives: 69.5 us -> 0 us
  Pallas kernels: 0 us -> 25.9 us
  starting transfers between devices: 0.04 us -> 21.2 us
  between operations: 13.5 us -> 0.13 us
  local copies, waits for them, and re-layouts: 15.5 us -> 4.78 us
  other arithmetic: 9.16 us -> 2.49 us
  matrix products: 6.37 us -> 0 us
    all_to_all x1 -> x0, blocking collectives: 69.5 us -> none  [body(): lax.all_to_all(projections, 'dp', split_axis=2, concat_axis=1, tiled=True)]
    pallas_call x0 -> x10, Pallas kernels: none -> 25.9 us  [call(): pl.pallas_call(kernel, name=name, grid_spec=pltpu.PrefetchScalarGridSpec(...]
    ppermute x0 -> x19, waiting for transfers between devices: none -> 23.3 us  [the longest x3 8.67 us: body(): sq_others = [lax.ppermute(sq, 'dp', xor_pairs(n_dp, b)) for b in (1, 2, 3)]]
    all_gather x2 -> x0, waiting for transfers between devices: 22 us -> none  [the longest x1 22 us: entering(): pieces = lax.all_gather(value, axis)]
    ppermute x0 -> x19, starting transfers between devices: none -> 21.2 us  [the longest x3 4.45 us: entering(): lax.ppermute(sent, 'ctx', xor_pairs(n_ctx, 2 * span * bits)).astype(F32)]
    all_to_all x2 -> x0, local copies, waits for them, and re-layouts: 6.93 us -> none  [body(): lax.all_to_all(projections, 'dp', split_axis=2, concat_axis=1, tiled=True)]
    select_n x7 -> x0, other arithmetic: 6.65 us -> none  [turn(): return jnp.where(position < mine, longer, subtotal)]
    dot_general x4 -> x0, matrix products: 6.37 us -> none  [the longest x1 4.42 us: body(): jnp.einsum('td,pdc->ptc', normed, mine, preferred_element_type=jnp.float32)]
  transfers between devices with their start and end apart: 2 -> 19, of which waited for: 1 -> 10; matrix products, arithmetic and copies ran while one was open for 8% -> 0% of each run, Pallas kernels for 0% -> 24%
where the time goes in v1:
time: 78.3 us; the launch traced here: 77.8 us
  Pallas kernels  25.9 us (33%)
  waiting for transfers between devices  23.3 us (30%)
  starting transfers between devices  21.2 us (27%)
  local copies, waits for them, and re-layouts  4.78 us (6%)
  other arithmetic  2.49 us (3%)
    pallas_call x10, Pallas kernels, call(): pl.pallas_call(kernel, name=name, grid_spec=pltpu.PrefetchScalarGridSpec(...  25.9 us
    ppermute x3, waiting for transfers between devices, body(): sq_others = [lax.ppermute(sq, 'dp', xor_pairs(n_dp, b)) for b in (1, 2, 3)]  8.67 us
    ppermute x3, waiting for transfers between devices, entering(): lax.ppermute(sent, 'ctx', xor_pairs(n_ctx, 2 * span * bits)).astype(F32)  5.49 us
    unnamed x30, local copies, waits for them, and re-layouts  4.78 us
    ppermute x3, starting transfers between devices, entering(): lax.ppermute(sent, 'ctx', xor_pairs(n_ctx, 2 * span * bits)).astype(F32)  4.45 us
    ppermute x3, starting transfers between devices, body(): sq_others = [lax.ppermute(sq, 'dp', xor_pairs(n_dp, b)) for b in (1, 2, 3)]  4.08 us
    ppermute x2, starting transfers between devices, first(): lax.ppermute(s0, 'dp', xor_pairs(n_dp, 1))  3.5 us
    ppermute x3, starting transfers between devices, body(): lax.ppermute(s, 'dp', xor_pairs(n_dp, b))  3.49 us
  transfers between devices with their start and end apart: 19, of which 10 were waited for; matrix products, arithmetic and copies ran while one was open for 0% of the time, Pallas kernels for 24%

profile of v1, /device:TPU:0, one launch (start us, length us, event | category | flops | bytes accessed | tf_op | source)
XLA Modules:
  0.0 77.8 jit_solution(5788096250983971722)
XLA Ops:
  0.0 2.7 %first_k.1 = (bf16[512,256]{1,0:T(8,128)(2,1)}, bf16[512,256]{1,0:T(8,128)(2,1)}) custom-call(s32[1]{0:T(128)} %bitcast.m, bf16[512,512]{1,0:T(8,128)(2,1)} %x.15, f32[1,2048]{1,0:T(1,128)} %bitcast.16, bf16[3,512,1024]{2,1,0:T(8,128)(2,1)} %wq.1, bf16[3,512,1024]{2,1,0:T(8,128)(2,1)} %wq.1, bf16[3,512,1024]{2,1,0:T(8,128)(2,1)} %wq.1, bf16[3,512,1024]{2,1,0:T(8,128)(2,1)} %wq.1), custom_call_target="tpu_custom_call" | custom-call | flops 268435456 | bytes 1056768 | tf_op jit(solution)/shard_map/first_k/pallas_call | solution.py:61
  2.7 3.0 %collective-permute-start.3 = (bf16[512,256]{1,0:T(8,128)(2,1)}, bf16[512,256]{1,0:T(8,128)(2,1)S(1)}, u32[]{:S(2)}, u32[]{:S(2)}) collective-permute-start(bf16[512,256]{1,0:T(8,128)(2,1)} %get-tuple-element.23), channel_id=1, source_target_pairs={{0,8},{8,0},{16,24},{24,16},{1,9},{9,1},{17,25},{25,17},{2,10},{10... | collective-permute-start | bytes 786440 | tf_op jit(solution)/shard_map/ppermute | solution.py:93
  5.6 1.5 %collective-permute-start.4 = (bf16[512,256]{1,0:T(8,128)(2,1)}, bf16[512,256]{1,0:T(8,128)(2,1)S(1)}, u32[]{:S(2)}, u32[]{:S(2)}) collective-permute-start(bf16[512,256]{1,0:T(8,128)(2,1)} %get-tuple-element.24), channel_id=1, source_target_pairs={{0,16},{8,24},{16,0},{24,8},{1,17},{9,25},{17,1},{25,9},{2,18},{10... | collective-permute-start | bytes 786440 | tf_op jit(solution)/shard_map/ppermute | solution.py:93
  7.1 2.6 %first_v.1 = (bf16[512,256]{1,0:T(8,128)(2,1)}, bf16[512,256]{1,0:T(8,128)(2,1)}) custom-call(s32[1]{0:T(128)} %bitcast.m, bf16[512,512]{1,0:T(8,128)(2,1)} %x.15, f32[1,2048]{1,0:T(1,128)} %bitcast.17, bf16[3,512,1024]{2,1,0:T(8,128)(2,1)} %wq.1, bf16[3,512,1024]{2,1,0:T(8,128)(2,1)} %wq.1, bf16[3,512,1024]{2,1,0:T(8,128)(2,1)} %wq.1, bf16[3,512,1024]{2,1,0:T(8,128)(2,1)} %wq.1), custom_call_target="tpu_custom_call" | custom-call | flops 268435456 | bytes 1056768 | tf_op jit(solution)/shard_map/first_v/pallas_call | solution.py:61
  9.8 0.5 collective-permute-start.7
  10.3 0.0 collective-permute-start.8
  10.3 2.3 %collective-permute-done.3.r0.ka0 = bf16[512,256]{1,0:T(8,128)(2,1)S(1)} collective-permute-done((bf16[512,256]{1,0:T(8,128)(2,1)}, bf16[512,256]{1,0:T(8,128)(2,1)S(1)}, u32[]{:S(2)}, u32[]{:S(2)}) %collective-permute-start.3) | collective-permute-done | bytes 262176 | tf_op jit(solution)/shard_map/ppermute | solution.py:93
  12.6 2.4 %collective-permute-done.4.r1.ka1 = bf16[512,256]{1,0:T(8,128)(2,1)S(1)} collective-permute-done((bf16[512,256]{1,0:T(8,128)(2,1)}, bf16[512,256]{1,0:T(8,128)(2,1)S(1)}, u32[]{:S(2)}, u32[]{:S(2)}) %collective-permute-start.4) | collective-permute-done | bytes 262176 | tf_op jit(solution)/shard_map/ppermute | solution.py:93
  15.0 0.7 copy-done.1
  15.7 2.4 %second_k.1 = (bf16[512,128]{1,0:T(8,128)(2,1)}, bf16[512,128]{1,0:T(8,128)(2,1)}) custom-call(s32[1]{0:T(128)} %bitcast.m, bf16[512,512]{1,0:T(8,128)(2,1)} %x.15, f32[1,2048]{1,0:T(1,128)} %bitcast.18, bf16[3,512,1024]{2,1,0:T(8,128)(2,1)} %wq.1, bf16[3,512,1024]{2,1,0:T(8,128)(2,1)} %wq.1, bf16[512,256]{1,0:T(8,128)(2,1)} %copy-done, ...), custom_call_target="tpu_custom_call" | custom-call | flops 134217728 | bytes 1318912 | tf_op jit(solution)/shard_map/second_k/pallas_call | solution.py:61
  18.1 1.5 %collective-permute-start.5 = (bf16[512,128]{1,0:T(8,128)(2,1)}, bf16[512,128]{1,0:T(8,128)(2,1)S(1)}, u32[]{:S(2)}, u32[]{:S(2)}) collective-permute-start(bf16[512,128]{1,0:T(8,128)(2,1)} %get-tuple-element.25), channel_id=1, source_target_pairs={{0,16},{8,24},{16,0},{24,8},{1,17},{9,25},{17,1},{25,9},{2,18},{10... | collective-permute-start | bytes 393224 | tf_op jit(solution)/shard_map/ppermute | solution.py:118
  19.6 0.7 collective-permute-start.6
  20.3 0.0 collective-permute-done.7.va0.r0
  20.3 0.0 collective-permute-done.8.va1.r1
  20.3 0.7 copy-done.2
  21.0 0.7 copy-done.3
  21.7 2.4 %second_v.1 = (bf16[512,128]{1,0:T(8,128)(2,1)}, bf16[512,128]{1,0:T(8,128)(2,1)}) custom-call(s32[1]{0:T(128)} %bitcast.m, bf16[512,512]{1,0:T(8,128)(2,1)} %x.15, f32[1,2048]{1,0:T(1,128)} %bitcast.19, bf16[3,512,1024]{2,1,0:T(8,128)(2,1)} %wq.1, bf16[3,512,1024]{2,1,0:T(8,128)(2,1)} %wq.1, bf16[512,256]{1,0:T(8,128)(2,1)} %copy-done.2, ...), custom_call_target="tpu_custom_call" | custom-call | flops 134217728 | bytes 1318912 | tf_op jit(solution)/shard_map/second_v/pallas_call | solution.py:61
  24.1 0.7 collective-permute-start.12
  24.8 1.1 %collective-permute-start.13 = (bf16[512,128]{1,0:T(8,128)(2,1)}, bf16[512,128]{1,0:T(8,128)(2,1)S(1)}, u32[]{:S(2)}, u32[]{:S(2)}) collective-permute-start(bf16[512,128]{1,0:T(8,128)(2,1)} %get-tuple-element.36), channel_id=1, source_target_pairs={{0,8},{8,0},{16,24},{24,16},{1,9},{9,1},{17,25},{25,17},{2,10},{10... | collective-permute-start | bytes 393224 | tf_op jit(solution)/shard_map/ppermute | solution.py:118
  26.0 2.1 %squares.1.s0 = f32[8,512]{1,0:T(8,128)} custom-call(s32[1]{0:T(128)} %bitcast.m, bf16[512,512]{1,0:T(8,128)(2,1)} %x.15), custom_call_target="tpu_custom_call" | custom-call | flops 8388608 | bytes 540672 | tf_op jit(solution)/shard_map/squares/pallas_call | solution.py:61
  28.0 0.9 %collective-permute-start = (f32[8,512]{1,0:T(8,128)}, f32[8,512]{1,0:T(8,128)S(1)}, u32[]{:S(2)}, u32[]{:S(2)}) collective-permute-start(f32[8,512]{1,0:T(8,128)} %squares.1.s0), channel_id=1, source_target_pairs={{0,8},{8,0},{16,24},{24,16},{1,9},{9,1},{17,25},{25,17},{2,10},{10... | collective-permute-start | bytes 49160 | tf_op jit(solution)/shard_map/ppermute | solution.py:108
  28.9 3.0 %collective-permute-done.s1 = f32[8,512]{1,0:T(8,128)S(1)} collective-permute-done((f32[8,512]{1,0:T(8,128)}, f32[8,512]{1,0:T(8,128)S(1)}, u32[]{:S(2)}, u32[]{:S(2)}) %collective-permute-start) | collective-permute-done | bytes 16416 | tf_op jit(solution)/shard_map/ppermute | solution.py:108
  32.0 1.5 %collective-permute-start.1 = (f32[8,512]{1,0:T(8,128)}, f32[8,512]{1,0:T(8,128)S(1)}, u32[]{:S(2)}, u32[]{:S(2)}) collective-permute-start(f32[8,512]{1,0:T(8,128)} %squares.1.s0), channel_id=1, source_target_pairs={{0,16},{8,24},{16,0},{24,8},{1,17},{9,25},{17,1},{25,9},{2,18},{10... | collective-permute-start | bytes 49160 | tf_op jit(solution)/shard_map/ppermute | solution.py:108
  33.5 2.4 %collective-permute-done.1.s2 = f32[8,512]{1,0:T(8,128)S(1)} collective-permute-done((f32[8,512]{1,0:T(8,128)}, f32[8,512]{1,0:T(8,128)S(1)}, u32[]{:S(2)}, u32[]{:S(2)}) %collective-permute-start.1) | collective-permute-done | bytes 16416 | tf_op jit(solution)/shard_map/ppermute | solution.py:108
  35.9 1.6 %collective-permute-start.2 = (f32[8,512]{1,0:T(8,128)}, f32[8,512]{1,0:T(8,128)S(1)}, u32[]{:S(2)}, u32[]{:S(2)}) collective-permute-start(f32[8,512]{1,0:T(8,128)} %squares.1.s0), channel_id=1, source_target_pairs={{0,24},{8,16},{16,8},{24,0},{1,25},{9,17},{17,9},{25,1},{2,26},{10... | collective-permute-start | bytes 49160 | tf_op jit(solution)/shard_map/ppermute | solution.py:108
  37.6 3.2 %collective-permute-done.2.s3 = f32[8,512]{1,0:T(8,128)S(1)} collective-permute-done((f32[8,512]{1,0:T(8,128)}, f32[8,512]{1,0:T(8,128)S(1)}, u32[]{:S(2)}, u32[]{:S(2)}) %collective-permute-start.2) | collective-permute-done | bytes 16416 | tf_op jit(solution)/shard_map/ppermute | solution.py:108
  40.8 0.0 collective-permute-done.5.kb0
  40.8 0.0 collective-permute-done.6.kb1
  40.8 0.6 copy-done.14
  41.4 0.1 copy-done.8
  41.4 0.6 copy-done.9
  42.1 3.1 %keys.1 = (bf16[512,256]{1,0:T(8,128)(2,1)}, f32[512,256]{1,0:T(8,128)}, f32[512,128]{1,0:T(8,128)}) custom-call(s32[1]{0:T(128)} %bitcast.m, bf16[512,512]{1,0:T(8,128)(2,1)} %x.15, f32[1,2048]{1,0:T(1,128)} %bitcast.20, bf16[3,512,1024]{2,1,0:T(8,128)(2,1)} %wq.1, bf16[3,512,1024]{2,1,0:T(8,128)(2,1)} %wq.1, f32[8,512]{1,0:T(8,128)} %squares.1.s0, ...), custom_call_target="tpu_custom_call" | custom-call | flops 268435456 | bytes 2957312 | tf_op jit(solution)/shard_map/keys/pallas_call | solution.py:61
  45.2 0.0 collective-permute-done.12.b0
  45.2 0.0 copy-start.10
  45.2 0.0 collective-permute-done.13.b1
  45.2 0.0 copy-start.11
  45.2 0.6 copy-done.10
  45.8 0.0 copy-done.11
  45.9 2.2 %values.1 = (bf16[512,256]{1,0:T(8,128)(2,1)}, f32[2,128,128]{2,1,0:T(8,128)}) custom-call(s32[1]{0:T(128)} %bitcast.m, bf16[512,256]{1,0:T(8,128)(2,1)} %get-tuple-element.33.k, f32[512,256]{1,0:T(8,128)} %get-tuple-element.34.v, f32[512,128]{1,0:T(8,128)} %get-tuple-element.29.s, bf16[512,128]{1,0:T(8,128)(2,1)} %copy-done.10, bf16[512,128]{1,0:T(8,128)(2,1)} %copy-done.11), custom_call_target="tpu_custom_call" | custom-call | flops 33554432 | bytes 1703936 | tf_op jit(solution)/shard_map/values/pallas_call | solution.py:61
  48.1 0.9 %fusion.5 = bf16[128,128]{1,0:T(8,128)(2,1)S(1)} fusion(f32[2,128,128]{2,1,0:T(8,128)} %get-tuple-element.40, pred[]{:T(512)S(6)} %eq.5), kind=kLoop, calls=%fused_computation.12 | loop fusion | flops 16384 | bytes 98305 | tf_op jit(solution)/shard_map/convert_element_type | solution.py:209
  48.9 0.1 collective-permute-start.14
  49.0 1.2 %collective-permute-done.14 = bf16[128,128]{1,0:T(8,128)(2,1)S(1)} collective-permute-done((bf16[128,128]{1,0:T(8,128)(2,1)S(1)}, bf16[128,128]{1,0:T(8,128)(2,1)S(1)}, u32[]{:S(2)}, u32[]{:S(2)}) %collective-permute-start.14) | collective-permute-done | bytes 32800 | tf_op jit(solution)/shard_map/ppermute | solution.py:210
  50.2 0.9 %fusion = bf16[128,128]{1,0:T(8,128)(2,1)S(1)} fusion(bf16[128,128]{1,0:T(8,128)(2,1)S(1)} %collective-permute-done.14, f32[2,128,128]{2,1,0:T(8,128)} %get-tuple-element.40, pred[]{:T(512)S(6)} %eq.5), kind=kLoop, calls=%fused_computation.2 | loop fusion | flops 65536 | bytes 196609 | tf_op jit(solution)/shard_map/convert_element_type | solution.py:217
  51.1 1.6 %collective-permute-start.15 = (bf16[128,128]{1,0:T(8,128)(2,1)S(1)}, bf16[128,128]{1,0:T(8,128)(2,1)S(1)}, u32[]{:S(2)}, u32[]{:S(2)}) collective-permute-start(bf16[128,128]{1,0:T(8,128)(2,1)S(1)} %fusion), channel_id=1, source_target_pairs={{0,2},{1,3},{2,0},{3,1},{4,6},{5,7},{6,4},{7,5},{8,10},{9,11},{10,... | collective-permute-start | bytes 98312 | tf_op jit(solution)/shard_map/ppermute | solution.py:219
  52.8 2.7 %query.1 = (bf16[512,256]{1,0:T(8,128)(2,1)}, bf16[512,256]{1,0:T(8,128)(2,1)}, bf16[512,256]{1,0:T(8,128)(2,1)}) custom-call(s32[1]{0:T(128)} %bitcast.m, bf16[512,512]{1,0:T(8,128)(2,1)} %x.15, f32[1,2048]{1,0:T(1,128)} %bitcast.21, bf16[3,512,1024]{2,1,0:T(8,128)(2,1)} %wq.1, bf16[3,512,1024]{2,1,0:T(8,128)(2,1)} %wq.1, bf16[3,512,1024]{2,1,0:T(8,128)(2,1)} %wq.1), custom_call_target="tpu_custom_call" | custom-call | flops 402653184 | bytes 1318912 | tf_op jit(solution)/shard_map/query/pallas_call | solution.py:61
  55.4 1.5 %collective-permute-start.10 = (bf16[512,256]{1,0:T(8,128)(2,1)}, bf16[512,256]{1,0:T(8,128)(2,1)S(1)}, u32[]{:S(2)}, u32[]{:S(2)}) collective-permute-start(bf16[512,256]{1,0:T(8,128)(2,1)} %get-tuple-element.31), channel_id=1, source_target_pairs={{0,16},{8,24},{16,0},{24,8},{1,17},{9,25},{17,1},{25,9},{2,18},{10... | collective-permute-start | bytes 786440 | tf_op jit(solution)/shard_map/ppermute | solution.py:130
  57.0 0.9 %collective-permute-start.11 = (bf16[512,256]{1,0:T(8,128)(2,1)}, bf16[512,256]{1,0:T(8,128)(2,1)S(1)}, u32[]{:S(2)}, u32[]{:S(2)}) collective-permute-start(bf16[512,256]{1,0:T(8,128)(2,1)} %get-tuple-element.32), channel_id=1, source_target_pairs={{0,24},{8,16},{16,8},{24,0},{1,25},{9,17},{17,9},{25,1},{2,26},{10... | collective-permute-start | bytes 786440 | tf_op jit(solution)/shard_map/ppermute | solution.py:130
  57.8 1.1 %collective-permute-start.9 = (bf16[512,256]{1,0:T(8,128)(2,1)}, bf16[512,256]{1,0:T(8,128)(2,1)S(1)}, u32[]{:S(2)}, u32[]{:S(2)}) collective-permute-start(bf16[512,256]{1,0:T(8,128)(2,1)} %get-tuple-element.30), channel_id=1, source_target_pairs={{0,8},{8,0},{16,24},{24,16},{1,9},{9,1},{17,25},{25,17},{2,10},{10... | collective-permute-start | bytes 786440 | tf_op jit(solution)/shard_map/ppermute | solution.py:130
  58.9 2.6 %collective-permute-start.16 = (bf16[128,128]{1,0:T(8,128)(2,1)S(1)}, bf16[128,128]{1,0:T(8,128)(2,1)S(1)}, u32[]{:S(2)}, u32[]{:S(2)}) collective-permute-start(bf16[128,128]{1,0:T(8,128)(2,1)S(1)} %fusion), channel_id=1, source_target_pairs={{0,4},{1,5},{2,6},{3,7},{4,0},{5,1},{6,2},{7,3},{8,12},{9,13},{10,... | collective-permute-start | bytes 98312 | tf_op jit(solution)/shard_map/ppermute | solution.py:219
  61.5 0.0 collective-permute-done.15
  61.5 0.2 collective-permute-start.17
  61.7 2.2 %collective-permute-done.16 = bf16[128,128]{1,0:T(8,128)(2,1)S(1)} collective-permute-done((bf16[128,128]{1,0:T(8,128)(2,1)S(1)}, bf16[128,128]{1,0:T(8,128)(2,1)S(1)}, u32[]{:S(2)}, u32[]{:S(2)}) %collective-permute-start.16) | collective-permute-done | bytes 32800 | tf_op jit(solution)/shard_map/ppermute | solution.py:219
  64.0 3.3 %collective-permute-done.17 = bf16[128,128]{1,0:T(8,128)(2,1)S(1)} collective-permute-done((bf16[128,128]{1,0:T(8,128)(2,1)S(1)}, bf16[128,128]{1,0:T(8,128)(2,1)S(1)}, u32[]{:S(2)}, u32[]{:S(2)}) %collective-permute-start.17) | collective-permute-done | bytes 32800 | tf_op jit(solution)/shard_map/ppermute | solution.py:219
  67.2 0.0 copy-done.4
  67.3 0.1 collective-permute-start.18
  67.4 2.0 %collective-permute-done.10.r2 = bf16[512,256]{1,0:T(8,128)(2,1)S(1)} collective-permute-done((bf16[512,256]{1,0:T(8,128)(2,1)}, bf16[512,256]{1,0:T(8,128)(2,1)S(1)}, u32[]{:S(2)}, u32[]{:S(2)}) %collective-permute-start.10) | collective-permute-done | bytes 262176 | tf_op jit(solution)/shard_map/ppermute | solution.py:130
  69.4 0.0 collective-permute-done.11.r3
  69.4 1.2 %collective-permute-done.9.r1 = bf16[512,256]{1,0:T(8,128)(2,1)S(1)} collective-permute-done((bf16[512,256]{1,0:T(8,128)(2,1)}, bf16[512,256]{1,0:T(8,128)(2,1)S(1)}, u32[]{:S(2)}, u32[]{:S(2)}) %collective-permute-start.9) | collective-permute-done | bytes 262176 | tf_op jit(solution)/shard_map/ppermute | solution.py:130
  70.6 0.0 copy-done.5
  70.6 0.7 copy-done.7
  71.3 3.6 %inner.1 = (bf16[512,256]{1,0:T(8,128)(2,1)}, f32[512,256]{1,0:T(8,128)}) custom-call(s32[1]{0:T(128)} %bitcast.m, bf16[512,512]{1,0:T(8,128)(2,1)} %x.15, f32[1,2048]{1,0:T(1,128)} %bitcast.22, bf16[3,512,1024]{2,1,0:T(8,128)(2,1)} %wq.1, f32[512,128]{1,0:T(8,128)} %get-tuple-element.29.s, bf16[512,256]{1,0:T(8,128)(2,1)} %copy-done.7, ...), custom_call_target="tpu_custom_call" | custom-call | flops 402653184 | bytes 2891776 | tf_op jit(solution)/shard_map/inner/pallas_call | solution.py:61
  74.9 0.0 collective-permute-done.18
  75.0 0.6 pad_maximum_fusion.st
  75.6 2.2 %outer.1 = bf16[512,256]{1,0:T(8,128)(2,1)} custom-call(s32[1]{0:T(128)} %bitcast.m, bf16[512,256]{1,0:T(8,128)(2,1)} %get-tuple-element.38.q, f32[512,256]{1,0:T(8,128)} %get-tuple-element.39.inner, bf16[2,128,128]{2,1,0:T(8,128)(2,1)} %pad_maximum_fusion.st, f32[1,256]{1,0:T(1,128)} %bitcast.23), custom_call_target="tpu_custom_call" | custom-call | flops 33554432 | bytes 1115136 | tf_op jit(solution)/shard_map/outer/pallas_call | solution.py:61
  (20 shorter events, 0.1 us)
Async XLA Ops:
  2.7 10.0 %collective-permute-start.3 = (bf16[512,256]{1,0:T(8,128)(2,1)}, bf16[512,256]{1,0:T(8,128)(2,1)S(1)}, u32[]{:S(2)}, u32[]{:S(2)}) collective-permute-start(bf16[512,256]{1,0:T(8,128)(2,1)} %get-tuple-element.23), channel_id=1, source_target_pairs={{0,8},{8,0},{16,24},{24,16},{1,9},{9,1},{17,25},{25,17},{2,10},{10... | collective-permute-start | bytes 786440 | tf_op jit(solution)/shard_map/ppermute | solution.py:93
  5.6 9.4 %collective-permute-start.4 = (bf16[512,256]{1,0:T(8,128)(2,1)}, bf16[512,256]{1,0:T(8,128)(2,1)S(1)}, u32[]{:S(2)}, u32[]{:S(2)}) collective-permute-start(bf16[512,256]{1,0:T(8,128)(2,1)} %get-tuple-element.24), channel_id=1, source_target_pairs={{0,16},{8,24},{16,0},{24,8},{1,17},{9,25},{17,1},{25,9},{2,18},{10... | collective-permute-start | bytes 786440 | tf_op jit(solution)/shard_map/ppermute | solution.py:93
  9.8 10.5 %collective-permute-start.7 = (bf16[512,256]{1,0:T(8,128)(2,1)}, bf16[512,256]{1,0:T(8,128)(2,1)S(1)}, u32[]{:S(2)}, u32[]{:S(2)}) collective-permute-start(bf16[512,256]{1,0:T(8,128)(2,1)} %get-tuple-element.27), channel_id=1, source_target_pairs={{0,8},{8,0},{16,24},{24,16},{1,9},{9,1},{17,25},{25,17},{2,10},{10... | collective-permute-start | bytes 786440 | tf_op jit(solution)/shard_map/ppermute | solution.py:93
  10.3 10.0 %collective-permute-start.8 = (bf16[512,256]{1,0:T(8,128)(2,1)}, bf16[512,256]{1,0:T(8,128)(2,1)S(1)}, u32[]{:S(2)}, u32[]{:S(2)}) collective-permute-start(bf16[512,256]{1,0:T(8,128)(2,1)} %get-tuple-element.28), channel_id=1, source_target_pairs={{0,16},{8,24},{16,0},{24,8},{1,17},{9,25},{17,1},{25,9},{2,18},{10... | collective-permute-start | bytes 786440 | tf_op jit(solution)/shard_map/ppermute | solution.py:93
  12.6 2.4 %copy-start = (bf16[512,256]{1,0:T(8,128)(2,1)}, bf16[512,256]{1,0:T(8,128)(2,1)S(1)}, u32[]{:S(2)}) copy-start(bf16[512,256]{1,0:T(8,128)(2,1)S(1)} %collective-permute-done.3.r0.ka0) | copy-start | bytes 786436
  15.0 0.7 copy-start.1
  18.1 22.7 %collective-permute-start.5 = (bf16[512,128]{1,0:T(8,128)(2,1)}, bf16[512,128]{1,0:T(8,128)(2,1)S(1)}, u32[]{:S(2)}, u32[]{:S(2)}) collective-permute-start(bf16[512,128]{1,0:T(8,128)(2,1)} %get-tuple-element.25), channel_id=1, source_target_pairs={{0,16},{8,24},{16,0},{24,8},{1,17},{9,25},{17,1},{25,9},{2,18},{10... | collective-permute-start | bytes 393224 | tf_op jit(solution)/shard_map/ppermute | solution.py:118
  19.6 21.2 %collective-permute-start.6 = (bf16[512,128]{1,0:T(8,128)(2,1)}, bf16[512,128]{1,0:T(8,128)(2,1)S(1)}, u32[]{:S(2)}, u32[]{:S(2)}) collective-permute-start(bf16[512,128]{1,0:T(8,128)(2,1)} %get-tuple-element.26), channel_id=1, source_target_pairs={{0,8},{8,0},{16,24},{24,16},{1,9},{9,1},{17,25},{25,17},{2,10},{10... | collective-permute-start | bytes 393224 | tf_op jit(solution)/shard_map/ppermute | solution.py:118
  20.3 0.7 copy-start.2
  21.0 0.7 copy-start.3
  24.1 21.1 %collective-permute-start.12 = (bf16[512,128]{1,0:T(8,128)(2,1)}, bf16[512,128]{1,0:T(8,128)(2,1)S(1)}, u32[]{:S(2)}, u32[]{:S(2)}) collective-permute-start(bf16[512,128]{1,0:T(8,128)(2,1)} %get-tuple-element.35), channel_id=1, source_target_pairs={{0,16},{8,24},{16,0},{24,8},{1,17},{9,25},{17,1},{25,9},{2,18},{10... | collective-permute-start | bytes 393224 | tf_op jit(solution)/shard_map/ppermute | solution.py:118
  24.8 20.4 %collective-permute-start.13 = (bf16[512,128]{1,0:T(8,128)(2,1)}, bf16[512,128]{1,0:T(8,128)(2,1)S(1)}, u32[]{:S(2)}, u32[]{:S(2)}) collective-permute-start(bf16[512,128]{1,0:T(8,128)(2,1)} %get-tuple-element.36), channel_id=1, source_target_pairs={{0,8},{8,0},{16,24},{24,16},{1,9},{9,1},{17,25},{25,17},{2,10},{10... | collective-permute-start | bytes 393224 | tf_op jit(solution)/shard_map/ppermute | solution.py:118
  28.0 3.9 %collective-permute-start = (f32[8,512]{1,0:T(8,128)}, f32[8,512]{1,0:T(8,128)S(1)}, u32[]{:S(2)}, u32[]{:S(2)}) collective-permute-start(f32[8,512]{1,0:T(8,128)} %squares.1.s0), channel_id=1, source_target_pairs={{0,8},{8,0},{16,24},{24,16},{1,9},{9,1},{17,25},{25,17},{2,10},{10... | collective-permute-start | bytes 49160 | tf_op jit(solution)/shard_map/ppermute | solution.py:108
  32.0 8.8 %copy-start.12 = (f32[8,512]{1,0:T(8,128)}, f32[8,512]{1,0:T(8,128)S(1)}, u32[]{:S(2)}) copy-start(f32[8,512]{1,0:T(8,128)S(1)} %collective-permute-done.s1) | copy-start | bytes 49156
  32.0 3.9 %collective-permute-start.1 = (f32[8,512]{1,0:T(8,128)}, f32[8,512]{1,0:T(8,128)S(1)}, u32[]{:S(2)}, u32[]{:S(2)}) collective-permute-start(f32[8,512]{1,0:T(8,128)} %squares.1.s0), channel_id=1, source_target_pairs={{0,16},{8,24},{16,0},{24,8},{1,17},{9,25},{17,1},{25,9},{2,18},{10... | collective-permute-start | bytes 49160 | tf_op jit(solution)/shard_map/ppermute | solution.py:108
  35.9 4.9 %copy-start.13 = (f32[8,512]{1,0:T(8,128)}, f32[8,512]{1,0:T(8,128)S(1)}, u32[]{:S(2)}) copy-start(f32[8,512]{1,0:T(8,128)S(1)} %collective-permute-done.1.s2) | copy-start | bytes 49156
  35.9 4.8 %collective-permute-start.2 = (f32[8,512]{1,0:T(8,128)}, f32[8,512]{1,0:T(8,128)S(1)}, u32[]{:S(2)}, u32[]{:S(2)}) collective-permute-start(f32[8,512]{1,0:T(8,128)} %squares.1.s0), channel_id=1, source_target_pairs={{0,24},{8,16},{16,8},{24,0},{1,25},{9,17},{17,9},{25,1},{2,26},{10... | collective-permute-start | bytes 49160 | tf_op jit(solution)/shard_map/ppermute | solution.py:108
  40.8 0.6 copy-start.14
  40.8 0.7 copy-start.8
  41.4 0.6 copy-start.9
  45.2 0.7 copy-start.10
  45.2 0.7 copy-start.11
  48.9 1.3 %collective-permute-start.14 = (bf16[128,128]{1,0:T(8,128)(2,1)S(1)}, bf16[128,128]{1,0:T(8,128)(2,1)S(1)}, u32[]{:S(2)}, u32[]{:S(2)}) collective-permute-start(bf16[128,128]{1,0:T(8,128)(2,1)S(1)} %fusion.5), channel_id=1, source_target_pairs={{0,1},{1,0},{2,3},{3,2},{4,5},{5,4},{6,7},{7,6},{8,9},{9,8},{10,11... | collective-permute-start | bytes 98312 | tf_op jit(solution)/shard_map/ppermute | solution.py:210
  51.1 16.1 %copy-start.4 = (f32[2,128,128]{2,1,0:T(8,128)S(1)}, f32[2,128,128]{2,1,0:T(8,128)}, u32[]{:S(2)}) copy-start(f32[2,128,128]{2,1,0:T(8,128)} %get-tuple-element.40) | copy-start | bytes 393220
  51.1 10.4 %collective-permute-start.15 = (bf16[128,128]{1,0:T(8,128)(2,1)S(1)}, bf16[128,128]{1,0:T(8,128)(2,1)S(1)}, u32[]{:S(2)}, u32[]{:S(2)}) collective-permute-start(bf16[128,128]{1,0:T(8,128)(2,1)S(1)} %fusion), channel_id=1, source_target_pairs={{0,2},{1,3},{2,0},{3,1},{4,6},{5,7},{6,4},{7,5},{8,10},{9,11},{10,... | collective-permute-start | bytes 98312 | tf_op jit(solution)/shard_map/ppermute | solution.py:219
  55.4 13.9 %collective-permute-start.10 = (bf16[512,256]{1,0:T(8,128)(2,1)}, bf16[512,256]{1,0:T(8,128)(2,1)S(1)}, u32[]{:S(2)}, u32[]{:S(2)}) collective-permute-start(bf16[512,256]{1,0:T(8,128)(2,1)} %get-tuple-element.31), channel_id=1, source_target_pairs={{0,16},{8,24},{16,0},{24,8},{1,17},{9,25},{17,1},{25,9},{2,18},{10... | collective-permute-start | bytes 786440 | tf_op jit(solution)/shard_map/ppermute | solution.py:130
  57.0 12.4 %collective-permute-start.11 = (bf16[512,256]{1,0:T(8,128)(2,1)}, bf16[512,256]{1,0:T(8,128)(2,1)S(1)}, u32[]{:S(2)}, u32[]{:S(2)}) collective-permute-start(bf16[512,256]{1,0:T(8,128)(2,1)} %get-tuple-element.32), channel_id=1, source_target_pairs={{0,24},{8,16},{16,8},{24,0},{1,25},{9,17},{17,9},{25,1},{2,26},{10... | collective-permute-start | bytes 786440 | tf_op jit(solution)/shard_map/ppermute | solution.py:130
  57.8 12.8 %collective-permute-start.9 = (bf16[512,256]{1,0:T(8,128)(2,1)}, bf16[512,256]{1,0:T(8,128)(2,1)S(1)}, u32[]{:S(2)}, u32[]{:S(2)}) collective-permute-start(bf16[512,256]{1,0:T(8,128)(2,1)} %get-tuple-element.30), channel_id=1, source_target_pairs={{0,8},{8,0},{16,24},{24,16},{1,9},{9,1},{17,25},{25,17},{2,10},{10... | collective-permute-start | bytes 786440 | tf_op jit(solution)/shard_map/ppermute | solution.py:130
  58.9 5.1 %collective-permute-start.16 = (bf16[128,128]{1,0:T(8,128)(2,1)S(1)}, bf16[128,128]{1,0:T(8,128)(2,1)S(1)}, u32[]{:S(2)}, u32[]{:S(2)}) collective-permute-start(bf16[128,128]{1,0:T(8,128)(2,1)S(1)} %fusion), channel_id=1, source_target_pairs={{0,4},{1,5},{2,6},{3,7},{4,0},{5,1},{6,2},{7,3},{8,12},{9,13},{10,... | collective-permute-start | bytes 98312 | tf_op jit(solution)/shard_map/ppermute | solution.py:219
  61.5 5.7 %collective-permute-start.17 = (bf16[128,128]{1,0:T(8,128)(2,1)S(1)}, bf16[128,128]{1,0:T(8,128)(2,1)S(1)}, u32[]{:S(2)}, u32[]{:S(2)}) collective-permute-start(bf16[128,128]{1,0:T(8,128)(2,1)S(1)} %fusion), channel_id=1, source_target_pairs={{0,6},{1,7},{2,4},{3,5},{4,2},{5,3},{6,0},{7,1},{8,14},{9,15},{10,... | collective-permute-start | bytes 98312 | tf_op jit(solution)/shard_map/ppermute | solution.py:219
  67.3 7.6 %collective-permute-start.18 = (bf16[128,128]{1,0:T(8,128)(2,1)S(1)}, bf16[128,128]{1,0:T(8,128)(2,1)S(1)}, u32[]{:S(2)}, u32[]{:S(2)}) collective-permute-start(bf16[128,128]{1,0:T(8,128)(2,1)S(1)} %fusion.4), channel_id=1, source_target_pairs={{0,1},{1,0},{2,3},{3,2},{4,5},{5,4},{6,7},{7,6},{8,9},{9,8},{10,11... | collective-permute-start | bytes 98312 | tf_op jit(solution)/shard_map/ppermute | solution.py:226
  69.4 1.2 %copy-start.5 = (bf16[512,256]{1,0:T(8,128)(2,1)}, bf16[512,256]{1,0:T(8,128)(2,1)S(1)}, u32[]{:S(2)}) copy-start(bf16[512,256]{1,0:T(8,128)(2,1)S(1)} %collective-permute-done.10.r2) | copy-start | bytes 786436
  69.4 1.2 %copy-start.6 = (bf16[512,256]{1,0:T(8,128)(2,1)}, bf16[512,256]{1,0:T(8,128)(2,1)S(1)}, u32[]{:S(2)}) copy-start(bf16[512,256]{1,0:T(8,128)(2,1)S(1)} %collective-permute-done.11.r3) | copy-start | bytes 786436
  70.6 0.7 copy-start.7

commit v2 on v0

v2 whole, which is shorter than its diff:
```python
import jax
import jax.numpy as jnp
from jax import lax
from jax.experimental import pallas as pl
from jax.experimental.pallas import tpu as pltpu
from jax.sharding import PartitionSpec as P

HEAD_DIM = 128
epsilon = 1e-05
F32 = jnp.float32
BF16 = jnp.bfloat16
Q, K, V = 0, 1, 2
VMEM_LIMIT = 8 * 2**20


def feature(inputs):
    return jnp.where(inputs > 0, inputs + 1.0, jnp.exp(jnp.minimum(inputs, 0.0)))


def mm(a, b):
    return jnp.dot(a, b, preferred_element_type=F32)


def swap(value, axis, bits):
    return lax.ppermute(value, axis, [(i, i ^ bits) for i in range(lax.axis_size(axis))])


def body(tokens, input_gain, projections, head_gain):
    steps, features = tokens.shape
    width = head_gain.shape[0]
    n_dp = lax.axis_size("dp")
    n_ctx = lax.axis_size("ctx")
    heads = width // HEAD_DIM
    total = features * n_dp
    columns = projections.shape[2]
    H = HEAD_DIM
    R = 16
    assert n_dp == 4 and heads == 2 and n_ctx % 2 == 0 and steps % (2 * H) == 0 and steps <= 8 * H
    vmem = pl.BlockSpec(memory_space=pltpu.VMEM)
    hbm = pl.BlockSpec(memory_space=pltpu.HBM)

    def call(kernel, arrays, outs, flops, specs=None, scratch=()):
        moved = sum(s.size * s.dtype.itemsize for s in list(arrays) + list(outs))
        return pl.pallas_call(
            kernel,
            in_specs=specs or [vmem] * len(arrays),
            out_specs=[vmem] * len(outs),
            out_shape=outs,
            scratch_shapes=list(scratch),
            compiler_params=pltpu.CompilerParams(vmem_limit_bytes=VMEM_LIMIT),
            cost_estimate=pl.CostEstimate(flops=flops, bytes_accessed=moved, transcendentals=0),
        )(*arrays)

    def arr(*shape, dtype=BF16):
        return jax.ShapeDtypeStruct(shape, dtype)

    block = 2 * steps * features * H

    def cols(bits, slot=0, n=H):
        at = (lax.axis_index("dp").astype(jnp.int32) ^ bits) * width + slot * H
        return pl.ds(pl.multiple_of(at, H), n)

    def sum_rows(ss, lanes):
        hi = ss.astype(BF16).astype(F32)
        lo = ss - hi
        row = lax.broadcasted_iota(jnp.int32, (R, lanes), 0)
        out = jnp.zeros((R, lanes), F32)
        parts = steps // lanes
        for i in range(parts):
            at = slice(i * lanes, i * lanes + lanes)
            out = jnp.where(row == i, hi[:, at], out)
            out = jnp.where(row == parts + i, lo[:, at], out)
        return out.astype(BF16)

    def read_rows(rows, lanes):
        parts = steps // lanes
        rows = rows.astype(F32)
        pieces = [rows[i:i + 1, :] + rows[parts + i:parts + i + 1, :] for i in range(parts)]
        return jnp.concatenate(pieces, axis=1)

    def first(xg, w, o0, o1):
        o0[:steps, :H] = mm(xg, w[:, cols(1, 0)]).astype(BF16)
        o0[:steps, H:] = mm(xg, w[:, cols(3, 0)]).astype(BF16)
        o1[:, :H] = mm(xg, w[:, cols(2, 1)]).astype(BF16)
        o1[:, H:] = mm(xg, w[:, cols(3, 1)]).astype(BF16)

    def first_k_kernel(x_hbm, gain_hbm, w_hbm, o0, o1, o_xg, o_w, o_sq, x, gain, sem):
        cx = pltpu.make_async_copy(x_hbm, x, sem.at[0])
        cg = pltpu.make_async_copy(gain_hbm, gain, sem.at[1])
        cw = pltpu.make_async_copy(w_hbm.at[K], o_w, sem.at[2])
        cx.start()
        cg.start()
        cw.start()
        cx.wait()
        cg.wait()
        xf = x[...].astype(F32)
        at = lax.axis_index("dp").astype(jnp.int32) * features
        g = gain[:, pl.ds(pl.multiple_of(at, H), features)]
        xg = (xf * g).astype(BF16)
        o_xg[...] = xg
        sq = xf * xf
        hi = sq.astype(BF16)
        lo = (sq - hi.astype(F32)).astype(BF16)
        ones = jnp.ones((R, features), BF16)
        dims = (((1,), (1,)), ((), ()))
        ss = lax.dot_general(ones, hi, dims, preferred_element_type=F32) + lax.dot_general(ones, lo, dims, preferred_element_type=F32)
        o_sq[...] = ss
        o0[steps:, :] = sum_rows(ss, 2 * H)
        cw.wait()
        first(xg, o_w, o0, o1)

    outs = [arr(steps + R, 2 * H), arr(steps, 2 * H), arr(steps, features), arr(features, columns), arr(R, steps, dtype=F32)]
    specs = [hbm, hbm, hbm]
    scratch = [pltpu.VMEM((steps, features), BF16), pltpu.VMEM((1, total), F32), pltpu.SemaphoreType.DMA((3,))]
    in_hbm = [pltpu.with_memory_space_constraint(a, pltpu.HBM) for a in (tokens, input_gain.reshape(1, total), projections)]
    s0, s1, xg, w_k, sq = call(first_k_kernel, in_hbm, outs, 4 * block, specs, scratch)
    k1 = swap(s0, "dp", 1), swap(s1, "dp", 2)

    def first_v_kernel(xg, w_hbm, o0, o1, o_wv, o_wq, sem):
        cv = pltpu.make_async_copy(w_hbm.at[V], o_wv, sem.at[0])
        cq = pltpu.make_async_copy(w_hbm.at[Q], o_wq, sem.at[1])
        cv.start()
        cq.start()
        cv.wait()
        first(xg[...], o_wv, o0, o1)
        cq.wait()

    outs = [arr(steps, 2 * H), arr(steps, 2 * H), arr(features, columns), arr(features, columns)]
    s0, s1, w_v, w_q = call(first_v_kernel, [xg, in_hbm[2]], outs, 4 * block, [vmem, hbm], [pltpu.SemaphoreType.DMA((2,))])
    v1 = swap(s0, "dp", 1), swap(s1, "dp", 2)

    def onward_kernel(x, wk, wv, pass_k, pass_v):
        xg = x[...]
        for w, o in ((wk, pass_k), (wv, pass_v)):
            o[:, :H] = mm(xg, w[:, cols(2, 0)])
            o[:, H:] = mm(xg, w[:, cols(1, 1)])

    pass_k, pass_v = call(onward_kernel, [xg, w_k, w_v], [arr(steps, width, dtype=F32)] * 2, 4 * block)

    def rest_kernel(x, wk, wv, wq, own_k, own_v, own_q, q1, q2, q3):
        xg = x[...]
        for bits, o in ((1, q1), (2, q2), (3, q3)):
            o[...] = mm(xg, wq[:, cols(bits, 0, width)]).astype(BF16)
        for w, own in ((wk, own_k), (wv, own_v), (wq, own_q)):
            own[...] = mm(xg, w[:, cols(0, 0, width)])

    outs = [arr(steps, width, dtype=F32)] * 3 + [arr(steps, width)] * 3
    own_k, own_v, own_q, *sends = call(rest_kernel, [xg, w_k, w_v, w_q], outs, 12 * block)

    def second_k_kernel(p, r0, r1, sq, o0, o1):
        o0[:steps, :] = (p[:, :H] + r0[:steps, H:].astype(F32)).astype(BF16)
        o1[...] = (p[:, H:] + r1[:, H:].astype(F32)).astype(BF16)
        o0[steps:, :] = sum_rows(sq[...] + read_rows(r0[steps:, :], 2 * H), H)

    s0, s1 = call(second_k_kernel, [pass_k, *k1, sq], [arr(steps + R, H), arr(steps, H)], 0)
    k2 = swap(s0, "dp", 2), swap(s1, "dp", 1)

    def second_v_kernel(p, r0, r1, o0, o1):
        o0[...] = (p[:, :H] + r0[:, H:].astype(F32)).astype(BF16)
        o1[...] = (p[:, H:] + r1[:, H:].astype(F32)).astype(BF16)

    s0, s1 = call(second_v_kernel, [pass_v, v1[0], v1[1]], [arr(steps, H), arr(steps, H)], 0)
    v2 = swap(s0, "dp", 2), swap(s1, "dp", 1)
    q_others = [swap(s, "dp", b) for b, s in zip((1, 2, 3), sends)]

    def keys_kernel(own, a0, a1, b0, b1, sq, o_k, o_s):
        ss = sq[:1, :] + read_rows(a0[steps:, :], 2 * H) + read_rows(b0[steps:, :], H)
        inv = lax.rsqrt(ss * (1.0 / total) + epsilon)
        scale = jnp.broadcast_to(inv, (H, steps)).T
        o_s[...] = scale
        for h, (a, b) in enumerate(((a0, b0), (a1, b1))):
            at = slice(h * H, h * H + H)
            u = (own[:, at] + a[:steps, :H].astype(F32) + b[:steps, :].astype(F32)) * scale
            o_k[:, at] = feature(u).astype(BF16)

    keys, scale = call(keys_kernel, [own_k, *k1, *k2, sq], [arr(steps, width), arr(steps, H, dtype=F32)], 0)

    def values_kernel(k, own, a0, a1, b0, b1, s, o_v, o_own, o_give, st):
        for h, (a, b) in enumerate(((a0, b0), (a1, b1))):
            at = slice(h * H, h * H + H)
            val = ((own[:, at] + a[:, :H].astype(F32) + b[...].astype(F32)) * s[...]).astype(BF16)
            o_v[:, at] = val
            st[h] = lax.dot_general(k[:, at], val, (((0,), (0,)), ((), ())), preferred_element_type=F32)
        odd = lax.axis_index("ctx").astype(jnp.int32) & 1
        o_own[...] = st[odd]
        o_give[...] = st[1 - odd].astype(BF16)

    outs = [arr(steps, width), arr(H, H, dtype=F32), arr(H, H)]
    scratch = [pltpu.VMEM((heads, H, H), F32)]
    values, own, give = call(values_kernel, [keys, own_v, *v1, *v2, scale], outs, 4 * steps * H * H, None, scratch)
    partner = swap(give, "ctx", 1)
    group = own + partner.astype(F32)
    before = []
    chips, span = n_ctx // 2, 1
    while span < chips:
        radix = 4 if chips % (span * 4) == 0 else 2
        sent = group.astype(BF16)
        came = [swap(sent, "ctx", 2 * span * bits) for bits in range(1, radix)]
        low = (2 * span).bit_length() - 1
        last = span * radix == chips

        def combine_kernel(*refs, low=low, radix=radix, last=last):
            first, rest = refs[:2], refs[2:]
            came, rest = rest[:radix - 1], rest[radix - 1:]
            at = lax.axis_index("ctx").astype(jnp.int32)
            digit = (at >> low) & (radix - 1)
            earlier = [((digit ^ bits) < digit).astype(jnp.int32).astype(F32) for bits in range(1, radix)]
            total_before = sum(c[...].astype(F32) * e for c, e in zip(came, earlier))
            if not last:
                out_group, out_before = rest[-2:]
                if len(rest) == 3:
                    total_before = total_before + rest[0][...]
                out_before[...] = total_before
                out_group[...] = first[0][...] + first[1][...].astype(F32) + sum(c[...].astype(F32) for c in came)
                return
            out_theirs, out_ours = rest[-2:]
            own_ref, partner_ref = rest[:2] if len(rest) >= 4 else first
            if len(rest) > 2:
                total_before = total_before + rest[-3][...]
            odd = (at & 1).astype(F32)
            out_theirs[...] = (total_before + own_ref[...] * (1.0 - odd)).astype(BF16)
            out_ours[...] = (total_before + partner_ref[...].astype(F32) * odd).astype(BF16)

        start = [own, partner] if span == 1 else [group, jnp.zeros_like(partner)]
        extra = ([own, partner] if last and span > 1 else []) + before
        outs = [arr(H, H), arr(H, H)] if last else [arr(H, H, dtype=F32)] * 2
        result = call(combine_kernel, start + came + extra, outs, 0)
        if not last:
            group, before = result[0], [result[1]]
        span *= radix
    theirs, ours = result
    other = swap(theirs, "ctx", 1)

    def inner_kernel(own, r1, r2, r3, s, k, v, o_q, o_m):
        rows = lax.broadcasted_iota(jnp.int32, (steps, steps), 0)
        causal = rows >= lax.broadcasted_iota(jnp.int32, (steps, steps), 1)
        for h in range(heads):
            at = slice(h * H, h * H + H)
            u = own[:, at] + r1[:, at].astype(F32) + r2[:, at].astype(F32) + r3[:, at].astype(F32)
            q = feature(u * s[...]).astype(BF16)
            o_q[:, at] = q
            sc = lax.dot_general(q, k[:, at], (((1,), (1,)), ((), ())), preferred_element_type=F32)
            sc = jnp.where(causal, sc, 0.0).astype(BF16)
            o_m[:, at] = mm(sc, v[:, at])

    outs = [arr(steps, width), arr(steps, width, dtype=F32)]
    queries, inner = call(inner_kernel, [own_q, *q_others, scale, keys, values], outs, 8 * steps * steps * H)

    def outer_kernel(q, inner, ours, other, hg, o):
        odd = (lax.axis_index("ctx").astype(jnp.int32) & 1) == 1
        a, b = ours[...].astype(F32), other[...].astype(F32)
        prior = jnp.where(odd, b, a).astype(BF16), jnp.where(odd, a, b).astype(BF16)
        for h in range(heads):
            at = slice(h * H, h * H + H)
            mixed = inner[:, at] + mm(q[:, at], prior[h])
            factor = lax.rsqrt(jnp.mean(mixed * mixed, axis=-1, keepdims=True) + epsilon)
            o[:, at] = (mixed * factor * hg[:, at]).astype(BF16)

    (out,) = call(outer_kernel, [queries, inner, ours, other, head_gain.reshape(1, width)], [arr(steps, width)], 4 * steps * H * H)
    return out


def solution(mesh):
    in_specs = (P("ctx", "dp"), P(), P(None, "dp", None), P("dp"))
    out_specs = P("ctx", "dp")

    return jax.shard_map(body, mesh=mesh, in_specs=in_specs, out_specs=out_specs, check_vma=False)
```

time: 137 us -> 43.8 us (0.32)
  blocking collectives: 69.5 us -> 0 us
  starting transfers between devices: 0.04 us -> 20.7 us
  local copies, waits for them, and re-layouts: 15.5 us -> 0.01 us
  between operations: 13.5 us -> 0.13 us
  other arithmetic: 9.16 us -> 0.01 us
  Pallas kernels: 0 us -> 8.69 us
  waiting for transfers between devices: 22.7 us -> 14.1 us
  matrix products: 6.37 us -> 0 us
    all_to_all x1 -> x0, blocking collectives: 69.5 us -> none  [body(): lax.all_to_all(projections, 'dp', split_axis=2, concat_axis=1, tiled=True)]
    all_gather x2 -> x0, waiting for transfers between devices: 22 us -> none  [the longest x1 22 us: entering(): pieces = lax.all_gather(value, axis)]
    ppermute x0 -> x16, starting transfers between devices: none -> 20.7 us  [swap(): lax.ppermute(value, axis, [(i, i ^ bits) for i in range(lax.axis_size(axi...]
    ppermute x0 -> x16, waiting for transfers between devices: none -> 14.1 us  [swap(): lax.ppermute(value, axis, [(i, i ^ bits) for i in range(lax.axis_size(axi...]
    pallas_call x0 -> x11, Pallas kernels: none -> 8.69 us  [call(): pl.pallas_call(kernel, in_specs=specs or [vmem] * len(arrays), out_specs=...]
    unnamed x5 -> x2, local copies, waits for them, and re-layouts: 7.62 us -> 0.01 us
    all_to_all x2 -> x0, local copies, waits for them, and re-layouts: 6.93 us -> none  [body(): lax.all_to_all(projections, 'dp', split_axis=2, concat_axis=1, tiled=True)]
    select_n x7 -> x0, other arithmetic: 6.65 us -> none  [turn(): return jnp.where(position < mine, longer, subtotal)]
  transfers between devices with their start and end apart: 2 -> 16, of which waited for: 1 -> 7; matrix products, arithmetic and copies ran while one was open for 8% -> 0% of each run, Pallas kernels for 0% -> 11%
where the time goes in v2:
time: 43.8 us; the launch traced here: 43.7 us
  starting transfers between devices  20.7 us (47%)
  waiting for transfers between devices  14.1 us (32%)
  Pallas kernels  8.69 us (20%)
    ppermute x16, starting transfers between devices, swap(): lax.ppermute(value, axis, [(i, i ^ bits) for i in range(lax.axis_size(axi...  20.7 us
    ppermute x16, waiting for transfers between devices, swap(): lax.ppermute(value, axis, [(i, i ^ bits) for i in range(lax.axis_size(axi...  14.1 us
    pallas_call x11, Pallas kernels, call(): pl.pallas_call(kernel, in_specs=specs or [vmem] * len(arrays), out_specs=...  8.69 us
  transfers between devices with their start and end apart: 16, of which 7 were waited for; matrix products, arithmetic and copies ran while one was open for 0% of the time, Pallas kernels for 11%

profile of v2, /device:TPU:0, one launch (start us, length us, event | category | flops | bytes accessed | tf_op | source)
XLA Modules:
  0.0 43.7 jit_solution(322678063312335793)
XLA Ops:
  0.0 2.3 %shard_map.46 = (bf16[528,256]{1,0:T(8,128)(2,1)S(1)}, bf16[512,256]{1,0:T(8,128)(2,1)S(1)}, bf16[512,512]{1,0:T(8,128)(2,1)S(1)}, bf16[512,1024]{1,0:T(8,128)(2,1)S(1)}, f32[16,512]{1,0:T(8,128)S(1)}) custom-call(bf16[512,512]{1,0:T(8,128)(2,1)} %x_hbm.1, f32[1,2048]{1,0:T(1,128)} %bitcast.3, bf16[3,512,1024]{2,1,0:T(8,128)(2,1)} %w_hbm.3), custom_call_target="tpu_custom_call" | custom-call | flops 268435456 | bytes 5816320 | tf_op jit(solution)/shard_map/pallas_call | solution.py:44
  2.3 3.0 %collective-permute-start.3 = (bf16[528,256]{1,0:T(8,128)(2,1)S(1)}, bf16[528,256]{1,0:T(8,128)(2,1)S(1)}, u32[]{:S(2)}, u32[]{:S(2)}) collective-permute-start(bf16[528,256]{1,0:T(8,128)(2,1)S(1)} %get-tuple-element.44), channel_id=1, source_target_pairs={{0,8},{8,0},{16,24},{24,16},{1,9},{9,1},{17,25},{25,17},{2,10},{10... | collective-permute-start | bytes 811016 | tf_op jit(solution)/shard_map/ppermute | solution.py:25
  5.3 1.5 %collective-permute-start.4 = (bf16[512,256]{1,0:T(8,128)(2,1)S(1)}, bf16[512,256]{1,0:T(8,128)(2,1)S(1)}, u32[]{:S(2)}, u32[]{:S(2)}) collective-permute-start(bf16[512,256]{1,0:T(8,128)(2,1)S(1)} %get-tuple-element.45), channel_id=1, source_target_pairs={{0,16},{8,24},{16,0},{24,8},{1,17},{9,25},{17,1},{25,9},{2,18},{10... | collective-permute-start | bytes 786440 | tf_op jit(solution)/shard_map/ppermute | solution.py:25
  6.9 2.0 %shard_map.47 = (bf16[512,256]{1,0:T(8,128)(2,1)S(1)}, bf16[512,256]{1,0:T(8,128)(2,1)S(1)}, bf16[512,1024]{1,0:T(8,128)(2,1)S(1)}, bf16[512,1024]{1,0:T(8,128)(2,1)S(1)}) custom-call(bf16[512,512]{1,0:T(8,128)(2,1)S(1)} %get-tuple-element.35.xg.x, bf16[3,512,1024]{2,1,0:T(8,128)(2,1)} %w_hbm.3), custom_call_target="tpu_custom_call" | custom-call | flops 268435456 | bytes 6291456 | tf_op jit(solution)/shard_map/pallas_call | solution.py:44
  8.8 0.6 %collective-permute-start.7 = (bf16[512,256]{1,0:T(8,128)(2,1)S(1)}, bf16[512,256]{1,0:T(8,128)(2,1)S(1)}, u32[]{:S(2)}, u32[]{:S(2)}) collective-permute-start(bf16[512,256]{1,0:T(8,128)(2,1)S(1)} %get-tuple-element.53), channel_id=1, source_target_pairs={{0,8},{8,0},{16,24},{24,16},{1,9},{9,1},{17,25},{25,17},{2,10},{10... | collective-permute-start | bytes 786440 | tf_op jit(solution)/shard_map/ppermute | solution.py:25
  9.4 0.1 collective-permute-start.8
  9.5 0.7 %shard_map.49 = (f32[512,256]{1,0:T(8,128)S(1)}, f32[512,256]{1,0:T(8,128)S(1)}) custom-call(bf16[512,512]{1,0:T(8,128)(2,1)S(1)} %get-tuple-element.35.xg.x, bf16[512,1024]{1,0:T(8,128)(2,1)S(1)} %get-tuple-element.36.wk, bf16[512,1024]{1,0:T(8,128)(2,1)S(1)} %get-tuple-element.37.wv), custom_call_target="tpu_custom_call" | custom-call | flops 268435456 | bytes 3670016 | tf_op jit(solution)/shard_map/pallas_call | solution.py:44
  10.2 4.3 %collective-permute-done.4.r1.a1 = bf16[512,256]{1,0:T(8,128)(2,1)S(1)} collective-permute-done((bf16[512,256]{1,0:T(8,128)(2,1)S(1)}, bf16[512,256]{1,0:T(8,128)(2,1)S(1)}, u32[]{:S(2)}, u32[]{:S(2)}) %collective-permute-start.4) | collective-permute-done | bytes 262176 | tf_op jit(solution)/shard_map/ppermute | solution.py:25
  14.5 0.0 collective-permute-done.3.r0.a0
  14.5 0.1 shard_map.50
  14.6 1.6 %collective-permute-start.5 = (bf16[528,128]{1,0:T(8,128)(2,1)S(1)}, bf16[528,128]{1,0:T(8,128)(2,1)S(1)}, u32[]{:S(2)}, u32[]{:S(2)}) collective-permute-start(bf16[528,128]{1,0:T(8,128)(2,1)S(1)} %get-tuple-element.48), channel_id=1, source_target_pairs={{0,16},{8,24},{16,0},{24,8},{1,17},{9,25},{17,1},{25,9},{2,18},{10... | collective-permute-start | bytes 405512 | tf_op jit(solution)/shard_map/ppermute | solution.py:25
  16.2 0.5 %collective-permute-start.6 = (bf16[512,128]{1,0:T(8,128)(2,1)S(1)}, bf16[512,128]{1,0:T(8,128)(2,1)S(1)}, u32[]{:S(2)}, u32[]{:S(2)}) collective-permute-start(bf16[512,128]{1,0:T(8,128)(2,1)S(1)} %get-tuple-element.49), channel_id=1, source_target_pairs={{0,8},{8,0},{16,24},{24,16},{1,9},{9,1},{17,25},{25,17},{2,10},{10... | collective-permute-start | bytes 393224 | tf_op jit(solution)/shard_map/ppermute | solution.py:25
  16.7 1.6 %collective-permute-done.7.r0.a0 = bf16[512,256]{1,0:T(8,128)(2,1)S(1)} collective-permute-done((bf16[512,256]{1,0:T(8,128)(2,1)S(1)}, bf16[512,256]{1,0:T(8,128)(2,1)S(1)}, u32[]{:S(2)}, u32[]{:S(2)}) %collective-permute-start.7) | collective-permute-done | bytes 262176 | tf_op jit(solution)/shard_map/ppermute | solution.py:25
  18.3 1.8 %collective-permute-done.8.r1.a1 = bf16[512,256]{1,0:T(8,128)(2,1)S(1)} collective-permute-done((bf16[512,256]{1,0:T(8,128)(2,1)S(1)}, bf16[512,256]{1,0:T(8,128)(2,1)S(1)}, u32[]{:S(2)}, u32[]{:S(2)}) %collective-permute-start.8) | collective-permute-done | bytes 262176 | tf_op jit(solution)/shard_map/ppermute | solution.py:25
  20.1 0.1 shard_map.52
  20.2 1.6 %collective-permute-start.9 = (bf16[512,128]{1,0:T(8,128)(2,1)S(1)}, bf16[512,128]{1,0:T(8,128)(2,1)S(1)}, u32[]{:S(2)}, u32[]{:S(2)}) collective-permute-start(bf16[512,128]{1,0:T(8,128)(2,1)S(1)} %get-tuple-element.56), channel_id=1, source_target_pairs={{0,16},{8,24},{16,0},{24,8},{1,17},{9,25},{17,1},{25,9},{2,18},{10... | collective-permute-start | bytes 393224 | tf_op jit(solution)/shard_map/ppermute | solution.py:25
  21.8 0.5 %collective-permute-start.10 = (bf16[512,128]{1,0:T(8,128)(2,1)S(1)}, bf16[512,128]{1,0:T(8,128)(2,1)S(1)}, u32[]{:S(2)}, u32[]{:S(2)}) collective-permute-start(bf16[512,128]{1,0:T(8,128)(2,1)S(1)} %get-tuple-element.57), channel_id=1, source_target_pairs={{0,8},{8,0},{16,24},{24,16},{1,9},{9,1},{17,25},{25,17},{2,10},{10... | collective-permute-start | bytes 393224 | tf_op jit(solution)/shard_map/ppermute | solution.py:25
  22.3 1.0 %shard_map.48 = (f32[512,256]{1,0:T(8,128)S(1)}, f32[512,256]{1,0:T(8,128)S(1)}, f32[512,256]{1,0:T(8,128)S(1)}, bf16[512,256]{1,0:T(8,128)(2,1)S(1)}, bf16[512,...) custom-call(bf16[512,512]{1,0:T(8,128)(2,1)S(1)} %get-tuple-element.35.xg.x, ...), custom_call_target="tpu_custom_call" | custom-call | flops 805306368 | bytes 6029312 | tf_op jit(solution)/shard_map/pallas_call | solution.py:44
  23.3 0.0 copy-start
  23.3 0.0 collective-permute-done.6.b1
  23.4 0.0 collective-permute-done.5.b0
  23.4 0.3 shard_map.51
  23.6 1.6 %collective-permute-done.9.b0 = bf16[512,128]{1,0:T(8,128)(2,1)S(1)} collective-permute-done((bf16[512,128]{1,0:T(8,128)(2,1)S(1)}, bf16[512,128]{1,0:T(8,128)(2,1)S(1)}, u32[]{:S(2)}, u32[]{:S(2)}) %collective-permute-start.9) | collective-permute-done | bytes 131104 | tf_op jit(solution)/shard_map/ppermute | solution.py:25
  25.3 1.5 %collective-permute-done.10.b1 = bf16[512,128]{1,0:T(8,128)(2,1)S(1)} collective-permute-done((bf16[512,128]{1,0:T(8,128)(2,1)S(1)}, bf16[512,128]{1,0:T(8,128)(2,1)S(1)}, u32[]{:S(2)}, u32[]{:S(2)}) %collective-permute-start.10) | collective-permute-done | bytes 131104 | tf_op jit(solution)/shard_map/ppermute | solution.py:25
  26.8 0.4 shard_map.53
  27.1 0.1 collective-permute-start.11
  27.2 0.6 %collective-permute-start = (bf16[512,256]{1,0:T(8,128)(2,1)S(1)}, bf16[512,256]{1,0:T(8,128)(2,1)S(1)}, u32[]{:S(2)}, u32[]{:S(2)}) collective-permute-start(bf16[512,256]{1,0:T(8,128)(2,1)S(1)} %get-tuple-element.40), channel_id=1, source_target_pairs={{0,8},{8,0},{16,24},{24,16},{1,9},{9,1},{17,25},{25,17},{2,10},{10... | collective-permute-start | bytes 786440 | tf_op jit(solution)/shard_map/ppermute | solution.py:25
  27.8 0.2 collective-permute-start.1
  28.0 2.8 %collective-permute-start.2 = (bf16[512,256]{1,0:T(8,128)(2,1)S(1)}, bf16[512,256]{1,0:T(8,128)(2,1)S(1)}, u32[]{:S(2)}, u32[]{:S(2)}) collective-permute-start(bf16[512,256]{1,0:T(8,128)(2,1)S(1)} %get-tuple-element.42), channel_id=1, source_target_pairs={{0,24},{8,16},{16,8},{24,0},{1,25},{9,17},{17,9},{25,1},{2,26},{10... | collective-permute-start | bytes 786440 | tf_op jit(solution)/shard_map/ppermute | solution.py:25
  30.8 0.0 collective-permute-done.11.refs_1_
  30.8 1.6 %collective-permute-start.12 = (bf16[128,128]{1,0:T(8,128)(2,1)S(1)}, bf16[128,128]{1,0:T(8,128)(2,1)S(1)}, u32[]{:S(2)}, u32[]{:S(2)}) collective-permute-start(bf16[128,128]{1,0:T(8,128)(2,1)S(1)} %add_convert_fusion), channel_id=1, source_target_pairs={{0,2},{1,3},{2,0},{3,1},{4,6},{5,7},{6,4},{7,5},{8,10},{9,11},{10,... | collective-permute-start | bytes 98312 | tf_op jit(solution)/shard_map/ppermute | solution.py:25
  32.4 2.6 %collective-permute-start.13 = (bf16[128,128]{1,0:T(8,128)(2,1)S(1)}, bf16[128,128]{1,0:T(8,128)(2,1)S(1)}, u32[]{:S(2)}, u32[]{:S(2)}) collective-permute-start(bf16[128,128]{1,0:T(8,128)(2,1)S(1)} %add_convert_fusion), channel_id=1, source_target_pairs={{0,4},{1,5},{2,6},{3,7},{4,0},{5,1},{6,2},{7,3},{8,12},{9,13},{10,... | collective-permute-start | bytes 98312 | tf_op jit(solution)/shard_map/ppermute | solution.py:25
  35.0 0.0 collective-permute-done.12.refs_2_
  35.0 3.4 %collective-permute-start.14 = (bf16[128,128]{1,0:T(8,128)(2,1)S(1)}, bf16[128,128]{1,0:T(8,128)(2,1)S(1)}, u32[]{:S(2)}, u32[]{:S(2)}) collective-permute-start(bf16[128,128]{1,0:T(8,128)(2,1)S(1)} %add_convert_fusion), channel_id=1, source_target_pairs={{0,6},{1,7},{2,4},{3,5},{4,2},{5,3},{6,0},{7,1},{8,14},{9,15},{10,... | collective-permute-start | bytes 98312 | tf_op jit(solution)/shard_map/ppermute | solution.py:25
  38.4 0.0 collective-permute-done.13.refs_3_
  38.4 2.3 %collective-permute-done.14.refs_4_ = bf16[128,128]{1,0:T(8,128)(2,1)S(1)} collective-permute-done((bf16[128,128]{1,0:T(8,128)(2,1)S(1)}, bf16[128,128]{1,0:T(8,128)(2,1)S(1)}, u32[]{:S(2)}, u32[]{:S(2)}) %collective-permute-start.14) | collective-permute-done | bytes 32800 | tf_op jit(solution)/shard_map/ppermute | solution.py:25
  40.8 0.1 collective-permute-start.15
  40.9 0.0 collective-permute-done.r1
  40.9 0.9 %collective-permute-done.1.r2 = bf16[512,256]{1,0:T(8,128)(2,1)S(1)} collective-permute-done((bf16[512,256]{1,0:T(8,128)(2,1)S(1)}, bf16[512,256]{1,0:T(8,128)(2,1)S(1)}, u32[]{:S(2)}, u32[]{:S(2)}) %collective-permute-start.1) | collective-permute-done | bytes 262176 | tf_op jit(solution)/shard_map/ppermute | solution.py:25
  41.8 0.0 collective-permute-done.2.r3
  41.8 0.8 %shard_map.54 = (bf16[512,256]{1,0:T(8,128)(2,1)S(1)}, f32[512,256]{1,0:T(8,128)S(1)}) custom-call(f32[512,256]{1,0:T(8,128)S(1)} %get-tuple-element.39.own, bf16[512,256]{1,0:T(8,128)(2,1)S(1)} %collective-permute-done.r1, bf16[512,256]{1,0:T(8,128)(2,1)S(1)} %collective-permute-done.1.r2, bf16[512,256]{1,0:T(8,128)(2,1)S(1)} %collective-permute-done.2.r3, ...), custom_call_target="tpu_custom_call" | custom-call | flops 268435456 | bytes 2883584 | tf_op jit(solution)/shard_map/pallas_call | solution.py:44
  42.6 0.0 collective-permute-done.15.other
  42.6 0.0 copy-done
  42.6 1.1 %shard_map.56 = bf16[512,256]{1,0:T(8,128)(2,1)} custom-call(bf16[512,256]{1,0:T(8,128)(2,1)S(1)} %get-tuple-element.59.q, f32[512,256]{1,0:T(8,128)S(1)} %get-tuple-element.60.inner, bf16[128,128]{1,0:T(8,128)(2,1)S(1)} %get-tuple-element.63.ours, bf16[128,128]{1,0:T(8,128)(2,1)S(1)} %collective-permute-done.15.other, f32[1,256]{1,0:T(1,128)S(1)} %bitcast.2), custom_call_target="tpu_custom_call" | custom-call | flops 33554432 | bytes 1115136 | tf_op jit(solution)/shard_map/pallas_call | solution.py:44
  (2 shorter events, 0.0 us)
Async XLA Ops:
  2.3 12.2 %collective-permute-start.3 = (bf16[528,256]{1,0:T(8,128)(2,1)S(1)}, bf16[528,256]{1,0:T(8,128)(2,1)S(1)}, u32[]{:S(2)}, u32[]{:S(2)}) collective-permute-start(bf16[528,256]{1,0:T(8,128)(2,1)S(1)} %get-tuple-element.44), channel_id=1, source_target_pairs={{0,8},{8,0},{16,24},{24,16},{1,9},{9,1},{17,25},{25,17},{2,10},{10... | collective-permute-start | bytes 811016 | tf_op jit(solution)/shard_map/ppermute | solution.py:25
  5.3 9.2 %collective-permute-start.4 = (bf16[512,256]{1,0:T(8,128)(2,1)S(1)}, bf16[512,256]{1,0:T(8,128)(2,1)S(1)}, u32[]{:S(2)}, u32[]{:S(2)}) collective-permute-start(bf16[512,256]{1,0:T(8,128)(2,1)S(1)} %get-tuple-element.45), channel_id=1, source_target_pairs={{0,16},{8,24},{16,0},{24,8},{1,17},{9,25},{17,1},{25,9},{2,18},{10... | collective-permute-start | bytes 786440 | tf_op jit(solution)/shard_map/ppermute | solution.py:25
  8.8 9.5 %collective-permute-start.7 = (bf16[512,256]{1,0:T(8,128)(2,1)S(1)}, bf16[512,256]{1,0:T(8,128)(2,1)S(1)}, u32[]{:S(2)}, u32[]{:S(2)}) collective-permute-start(bf16[512,256]{1,0:T(8,128)(2,1)S(1)} %get-tuple-element.53), channel_id=1, source_target_pairs={{0,8},{8,0},{16,24},{24,16},{1,9},{9,1},{17,25},{25,17},{2,10},{10... | collective-permute-start | bytes 786440 | tf_op jit(solution)/shard_map/ppermute | solution.py:25
  9.4 10.7 %collective-permute-start.8 = (bf16[512,256]{1,0:T(8,128)(2,1)S(1)}, bf16[512,256]{1,0:T(8,128)(2,1)S(1)}, u32[]{:S(2)}, u32[]{:S(2)}) collective-permute-start(bf16[512,256]{1,0:T(8,128)(2,1)S(1)} %get-tuple-element.54), channel_id=1, source_target_pairs={{0,16},{8,24},{16,0},{24,8},{1,17},{9,25},{17,1},{25,9},{2,18},{10... | collective-permute-start | bytes 786440 | tf_op jit(solution)/shard_map/ppermute | solution.py:25
  14.6 8.7 %collective-permute-start.5 = (bf16[528,128]{1,0:T(8,128)(2,1)S(1)}, bf16[528,128]{1,0:T(8,128)(2,1)S(1)}, u32[]{:S(2)}, u32[]{:S(2)}) collective-permute-start(bf16[528,128]{1,0:T(8,128)(2,1)S(1)} %get-tuple-element.48), channel_id=1, source_target_pairs={{0,16},{8,24},{16,0},{24,8},{1,17},{9,25},{17,1},{25,9},{2,18},{10... | collective-permute-start | bytes 405512 | tf_op jit(solution)/shard_map/ppermute | solution.py:25
  16.2 7.1 %collective-permute-start.6 = (bf16[512,128]{1,0:T(8,128)(2,1)S(1)}, bf16[512,128]{1,0:T(8,128)(2,1)S(1)}, u32[]{:S(2)}, u32[]{:S(2)}) collective-permute-start(bf16[512,128]{1,0:T(8,128)(2,1)S(1)} %get-tuple-element.49), channel_id=1, source_target_pairs={{0,8},{8,0},{16,24},{24,16},{1,9},{9,1},{17,25},{25,17},{2,10},{10... | collective-permute-start | bytes 393224 | tf_op jit(solution)/shard_map/ppermute | solution.py:25
  20.2 5.0 %collective-permute-start.9 = (bf16[512,128]{1,0:T(8,128)(2,1)S(1)}, bf16[512,128]{1,0:T(8,128)(2,1)S(1)}, u32[]{:S(2)}, u32[]{:S(2)}) collective-permute-start(bf16[512,128]{1,0:T(8,128)(2,1)S(1)} %get-tuple-element.56), channel_id=1, source_target_pairs={{0,16},{8,24},{16,0},{24,8},{1,17},{9,25},{17,1},{25,9},{2,18},{10... | collective-permute-start | bytes 393224 | tf_op jit(solution)/shard_map/ppermute | solution.py:25
  21.8 5.0 %collective-permute-start.10 = (bf16[512,128]{1,0:T(8,128)(2,1)S(1)}, bf16[512,128]{1,0:T(8,128)(2,1)S(1)}, u32[]{:S(2)}, u32[]{:S(2)}) collective-permute-start(bf16[512,128]{1,0:T(8,128)(2,1)S(1)} %get-tuple-element.57), channel_id=1, source_target_pairs={{0,8},{8,0},{16,24},{24,16},{1,9},{9,1},{17,25},{25,17},{2,10},{10... | collective-permute-start | bytes 393224 | tf_op jit(solution)/shard_map/ppermute | solution.py:25
  23.3 19.3 %copy-start = (f32[256]{0:T(256)S(1)}, f32[256]{0:T(256)}, u32[]{:S(2)}) copy-start(f32[256]{0:T(256)} %param.7) | copy-start | bytes 3076
  27.1 3.6 %collective-permute-start.11 = (bf16[128,128]{1,0:T(8,128)(2,1)S(1)}, bf16[128,128]{1,0:T(8,128)(2,1)S(1)}, u32[]{:S(2)}, u32[]{:S(2)}) collective-permute-start(bf16[128,128]{1,0:T(8,128)(2,1)S(1)} %get-tuple-element.62), channel_id=1, source_target_pairs={{0,1},{1,0},{2,3},{3,2},{4,5},{5,4},{6,7},{7,6},{8,9},{9,8},{10,11... | collective-permute-start | bytes 98312 | tf_op jit(solution)/shard_map/ppermute | solution.py:25
  27.2 13.6 %collective-permute-start = (bf16[512,256]{1,0:T(8,128)(2,1)S(1)}, bf16[512,256]{1,0:T(8,128)(2,1)S(1)}, u32[]{:S(2)}, u32[]{:S(2)}) collective-permute-start(bf16[512,256]{1,0:T(8,128)(2,1)S(1)} %get-tuple-element.40), channel_id=1, source_target_pairs={{0,8},{8,0},{16,24},{24,16},{1,9},{9,1},{17,25},{25,17},{2,10},{10... | collective-permute-start | bytes 786440 | tf_op jit(solution)/shard_map/ppermute | solution.py:25
  27.8 14.0 %collective-permute-start.1 = (bf16[512,256]{1,0:T(8,128)(2,1)S(1)}, bf16[512,256]{1,0:T(8,128)(2,1)S(1)}, u32[]{:S(2)}, u32[]{:S(2)}) collective-permute-start(bf16[512,256]{1,0:T(8,128)(2,1)S(1)} %get-tuple-element.41), channel_id=1, source_target_pairs={{0,16},{8,24},{16,0},{24,8},{1,17},{9,25},{17,1},{25,9},{2,18},{10... | collective-permute-start | bytes 786440 | tf_op jit(solution)/shard_map/ppermute | solution.py:25
  28.0 13.8 %collective-permute-start.2 = (bf16[512,256]{1,0:T(8,128)(2,1)S(1)}, bf16[512,256]{1,0:T(8,128)(2,1)S(1)}, u32[]{:S(2)}, u32[]{:S(2)}) collective-permute-start(bf16[512,256]{1,0:T(8,128)(2,1)S(1)} %get-tuple-element.42), channel_id=1, source_target_pairs={{0,24},{8,16},{16,8},{24,0},{1,25},{9,17},{17,9},{25,1},{2,26},{10... | collective-permute-start | bytes 786440 | tf_op jit(solution)/shard_map/ppermute | solution.py:25
  30.8 4.2 %collective-permute-start.12 = (bf16[128,128]{1,0:T(8,128)(2,1)S(1)}, bf16[128,128]{1,0:T(8,128)(2,1)S(1)}, u32[]{:S(2)}, u32[]{:S(2)}) collective-permute-start(bf16[128,128]{1,0:T(8,128)(2,1)S(1)} %add_convert_fusion), channel_id=1, source_target_pairs={{0,2},{1,3},{2,0},{3,1},{4,6},{5,7},{6,4},{7,5},{8,10},{9,11},{10,... | collective-permute-start | bytes 98312 | tf_op jit(solution)/shard_map/ppermute | solution.py:25
  32.4 6.0 %collective-permute-start.13 = (bf16[128,128]{1,0:T(8,128)(2,1)S(1)}, bf16[128,128]{1,0:T(8,128)(2,1)S(1)}, u32[]{:S(2)}, u32[]{:S(2)}) collective-permute-start(bf16[128,128]{1,0:T(8,128)(2,1)S(1)} %add_convert_fusion), channel_id=1, source_target_pairs={{0,4},{1,5},{2,6},{3,7},{4,0},{5,1},{6,2},{7,3},{8,12},{9,13},{10,... | collective-permute-start | bytes 98312 | tf_op jit(solution)/shard_map/ppermute | solution.py:25
  35.0 5.7 %collective-permute-start.14 = (bf16[128,128]{1,0:T(8,128)(2,1)S(1)}, bf16[128,128]{1,0:T(8,128)(2,1)S(1)}, u32[]{:S(2)}, u32[]{:S(2)}) collective-permute-start(bf16[128,128]{1,0:T(8,128)(2,1)S(1)} %add_convert_fusion), channel_id=1, source_target_pairs={{0,6},{1,7},{2,4},{3,5},{4,2},{5,3},{6,0},{7,1},{8,14},{9,15},{10,... | collective-permute-start | bytes 98312 | tf_op jit(solution)/shard_map/ppermute | solution.py:25
  40.8 1.8 %collective-permute-start.15 = (bf16[128,128]{1,0:T(8,128)(2,1)S(1)}, bf16[128,128]{1,0:T(8,128)(2,1)S(1)}, u32[]{:S(2)}, u32[]{:S(2)}) collective-permute-start(bf16[128,128]{1,0:T(8,128)(2,1)S(1)} %get-tuple-element.64), channel_id=1, source_target_pairs={{0,1},{1,0},{2,3},{3,2},{4,5},{5,4},{6,7},{7,6},{8,9},{9,8},{10,11... | collective-permute-start | bytes 98312 | tf_op jit(solution)/shard_map/ppermute | solution.py:25

commit v3 on v2

v3 whole, which is shorter than its diff:
```python
import jax
import jax.numpy as jnp
from jax import lax
from jax.experimental import pallas as pl
from jax.experimental.pallas import tpu as pltpu
from jax.sharding import PartitionSpec as P

HEAD_DIM = 128
epsilon = 1e-05
F32 = jnp.float32
BF16 = jnp.bfloat16
Q, K, V = 0, 1, 2
VMEM_LIMIT = 8 * 2**20
RADIX = 4


def feature(inputs):
    return jnp.where(inputs > 0, inputs + 1.0, jnp.exp(jnp.minimum(inputs, 0.0)))


def mm(a, b):
    return jnp.dot(a, b, preferred_element_type=F32)


def swap(value, axis, bits):
    return lax.ppermute(value, axis, [(i, i ^ bits) for i in range(lax.axis_size(axis))])


def swap_by_core(value, even_bits, odd_bits):
    n_dp, n_ctx = lax.axis_size("dp"), lax.axis_size("ctx")
    pairs = []
    for i in range(n_dp):
        for j in range(n_ctx):
            other = i ^ (odd_bits if j & 1 else even_bits)
            pairs.append((i * n_ctx + j, other * n_ctx + j))
    return lax.ppermute(value, ("dp", "ctx"), pairs)


def index(axis):
    return lax.axis_index(axis).astype(jnp.int32)


def first_hop():
    return 1 + (index("ctx") & 1)


def body(tokens, input_gain, projections, head_gain):
    steps, features = tokens.shape
    width = head_gain.shape[0]
    n_dp = lax.axis_size("dp")
    n_ctx = lax.axis_size("ctx")
    heads = width // HEAD_DIM
    total = features * n_dp
    columns = projections.shape[2]
    H = HEAD_DIM
    R = 16
    assert n_dp == 4 and heads == 2 and n_ctx % 2 == 0 and features % H == 0
    assert steps == 2 * width
    vmem = pl.BlockSpec(memory_space=pltpu.VMEM)
    hbm = pl.BlockSpec(memory_space=pltpu.HBM)

    def call(kernel, arrays, outs, flops, specs=None, scratch=()):
        moved = sum(s.size * s.dtype.itemsize for s in list(arrays) + list(outs))
        return pl.pallas_call(
            kernel,
            in_specs=specs or [vmem] * len(arrays),
            out_specs=[vmem] * len(outs),
            out_shape=outs,
            scratch_shapes=list(scratch),
            compiler_params=pltpu.CompilerParams(vmem_limit_bytes=VMEM_LIMIT),
            cost_estimate=pl.CostEstimate(flops=flops, bytes_accessed=moved, transcendentals=0),
        )(*arrays)

    def arr(*shape, dtype=BF16):
        return jax.ShapeDtypeStruct(shape, dtype)

    block = 2 * steps * features * H

    def cols(bits):
        return pl.ds(pl.multiple_of((index("dp") ^ bits) * width, width), width)

    def head_cols(bits, head):
        return pl.ds(pl.multiple_of((index("dp") ^ bits) * width + head * H, H), H)

    def squares(xf):
        sq = xf * xf
        hi = sq.astype(BF16)
        lo = (sq - hi.astype(F32)).astype(BF16)
        ones = jnp.ones((R, features), BF16)
        dims = (((1,), (1,)), ((), ()))
        return lax.dot_general(ones, hi, dims, preferred_element_type=F32) + lax.dot_general(ones, lo, dims, preferred_element_type=F32)

    def sum_rows(ss, lanes):
        hi = ss.astype(BF16).astype(F32)
        lo = ss - hi
        row = lax.broadcasted_iota(jnp.int32, (R, lanes), 0)
        out = jnp.zeros((R, lanes), F32)
        parts = steps // lanes
        for i in range(parts):
            at = slice(i * lanes, i * lanes + lanes)
            out = jnp.where(row == i, hi[:, at], out)
            out = jnp.where(row == parts + i, lo[:, at], out)
        return out.astype(BF16)

    def read_rows(rows, lanes):
        parts = steps // lanes
        rows = rows.astype(F32)
        pieces = [rows[i:i + 1, :] + rows[parts + i:parts + i + 1, :] for i in range(parts)]
        return pieces[0] if parts == 1 else jnp.concatenate(pieces, axis=1)

    C = width + H

    def first_1_kernel(x_hbm, gain_hbm, w_hbm, o, o_xg, o_wk, o_wv, o_sq, x, gain, sem):
        a = first_hop()
        copies = [pltpu.make_async_copy(x_hbm, x, sem.at[0]), pltpu.make_async_copy(gain_hbm, gain, sem.at[1])]
        for i, bits in enumerate((a, 3, 3 - a, 0)):
            at = cols(bits)
            copies.append(pltpu.make_async_copy(w_hbm.at[K, :, at], o_wk.at[:, at], sem.at[2 + 2 * i]))
            copies.append(pltpu.make_async_copy(w_hbm.at[V, :, at], o_wv.at[:, at], sem.at[3 + 2 * i]))
        for c in copies:
            c.start()
        copies[0].wait()
        copies[1].wait()
        xf = x[...].astype(F32)
        g = gain[:, pl.ds(pl.multiple_of(index("dp") * features, features), features)]
        xg = (xf * g).astype(BF16)
        o_xg[...] = xg
        ss = squares(xf)
        o_sq[...] = ss
        o[steps:, :2 * width] = sum_rows(ss, 2 * width)
        o[steps:, 2 * width:] = jnp.zeros((R, 2 * C - 2 * width), BF16)
        for i, bits in enumerate((a, 3)):
            copies[2 + 2 * i].wait()
            copies[3 + 2 * i].wait()
            at = i * C
            o[:steps, at:at + width] = mm(xg, o_wk[:, cols(bits)]).astype(BF16)
            o[:steps, at + width:at + C] = mm(xg, o_wv[:, head_cols(bits, 0)]).astype(BF16)
        for c in copies[6:]:
            c.wait()

    outs = [arr(steps + R, 2 * C), arr(steps, features), arr(features, columns), arr(features, columns), arr(R, steps, dtype=F32)]
    scratch = [pltpu.VMEM((steps, features), BF16), pltpu.VMEM((1, total), F32), pltpu.SemaphoreType.DMA((10,))]
    in_hbm = [pltpu.with_memory_space_constraint(a, pltpu.HBM) for a in (tokens, input_gain.reshape(1, total), projections)]
    s0, xg, w_k, w_v, sq = call(first_1_kernel, in_hbm, outs, 6 * block, [hbm] * 3, scratch)
    a1 = swap_by_core(s0, 1, 2)

    def first_2_kernel(x, wv, w_hbm, o, o_wq, sem):
        cq = pltpu.make_async_copy(w_hbm.at[Q], o_wq, sem.at[0])
        cq.start()
        xg = x[...]
        o[:, :H] = mm(xg, wv[:, head_cols(first_hop(), 1)]).astype(BF16)
        o[:, H:] = mm(xg, wv[:, head_cols(3, 1)]).astype(BF16)
        cq.wait()

    outs = [arr(steps, 2 * H), arr(features, columns)]
    s0, w_q = call(first_2_kernel, [xg, w_v, in_hbm[2]], outs, 2 * block, [vmem, vmem, hbm], [pltpu.SemaphoreType.DMA((1,))])
    b1 = swap_by_core(s0, 1, 2)

    def onward_kernel(x, wk, wv, pass_a, pass_b):
        xg = x[...]
        bits = 3 - first_hop()
        pass_a[:, :width] = mm(xg, wk[:, cols(bits)])
        v = mm(xg, wv[:, cols(bits)])
        pass_a[:, width:] = v[:, :H]
        pass_b[...] = v[:, H:]

    outs = [arr(steps, C, dtype=F32), arr(steps, H, dtype=F32)]
    pass_a, pass_b = call(onward_kernel, [xg, w_k, w_v], outs, 4 * block)

    def rest_kernel(x, wk, wv, wq, own_k, own_v, own_q, q1, q2, q3):
        xg = x[...]
        for bits, o in ((3 - first_hop(), q1), (first_hop(), q2), (3, q3)):
            o[...] = mm(xg, wq[:, cols(bits)]).astype(BF16)
        for w, own in ((wk, own_k), (wv, own_v), (wq, own_q)):
            own[...] = mm(xg, w[:, cols(0)])

    outs = [arr(steps, width, dtype=F32)] * 3 + [arr(steps, width)] * 3
    own_k, own_v, own_q, *sends = call(rest_kernel, [xg, w_k, w_v, w_q], outs, 12 * block)

    def second_1_kernel(p, r, sq, o):
        o[:steps, :] = (p[...] + r[:steps, C:].astype(F32)).astype(BF16)
        o[steps:, :width] = sum_rows(sq[...] + read_rows(r[steps:, :2 * width], 2 * width), width)
        o[steps:, width:] = jnp.zeros((R, H), BF16)

    (s0,) = call(second_1_kernel, [pass_a, a1, sq], [arr(steps + R, C)], 0)
    a2 = swap_by_core(s0, 2, 1)

    def second_2_kernel(p, r, o):
        o[...] = (p[...] + r[:, H:].astype(F32)).astype(BF16)

    (s0,) = call(second_2_kernel, [pass_b, b1], [arr(steps, H)], 0)
    b2 = swap_by_core(s0, 2, 1)
    q_others = [swap_by_core(sends[0], 2, 1), swap_by_core(sends[1], 1, 2), swap(sends[2], "dp", 3)]

    def state_of(k, v):
        return lax.dot_general(k, v, (((0,), (0,)), ((), ())), preferred_element_type=F32)

    def keys_kernel(own_k, own_v, a, b, sq, o_k, o_v, o_s, o_st):
        ss = sq[:1, :] + read_rows(a[steps:, :2 * width], 2 * width) + read_rows(b[steps:, :width], width)
        inv = lax.rsqrt(ss * (1.0 / total) + epsilon)
        scale = jnp.broadcast_to(inv, (H, steps)).T
        o_s[...] = scale
        for h in range(heads):
            at = slice(h * H, h * H + H)
            u = (own_k[:, at] + a[:steps, at].astype(F32) + b[:steps, at].astype(F32)) * scale
            o_k[:, at] = feature(u).astype(BF16)
        at = slice(width, C)
        val = ((own_v[:, :H] + a[:steps, at].astype(F32) + b[:steps, at].astype(F32)) * scale).astype(BF16)
        o_v[...] = val
        o_st[...] = state_of(o_k[:, :H], val)

    outs = [arr(steps, width), arr(steps, H), arr(steps, H, dtype=F32), arr(H, H, dtype=F32)]
    keys, values_0, scale, state_0 = call(keys_kernel, [own_k, own_v, a1, a2, sq], outs, 2 * steps * H * H)

    def values_kernel(k, own, a, b, s, st0, o_v, o_own, o_give):
        val = ((own[:, H:] + a[:, :H].astype(F32) + b[...].astype(F32)) * s[...]).astype(BF16)
        o_v[...] = val
        st1 = state_of(k[:, H:], val)
        odd = (index("ctx") & 1) == 1
        o_own[...] = jnp.where(odd, st1, st0[...])
        o_give[...] = jnp.where(odd, st0[...], st1).astype(BF16)

    outs = [arr(steps, H), arr(H, H, dtype=F32), arr(H, H)]
    values_1, own, give = call(values_kernel, [keys, own_v, b1, b2, scale, state_0], outs, 2 * steps * H * H)
    partner = swap(give, "ctx", 1)
    group = own + partner.astype(F32)
    before = []
    chips, span = n_ctx // 2, 1
    while span < chips:
        radix = RADIX if chips % (span * RADIX) == 0 else 2
        sent = group.astype(BF16)
        came = [swap(sent, "ctx", 2 * span * bits) for bits in range(1, radix)]
        low = (2 * span).bit_length() - 1
        last = span * radix == chips

        def combine_kernel(*refs, low=low, radix=radix, last=last):
            first, rest = refs[:2], refs[2:]
            came, rest = rest[:radix - 1], rest[radix - 1:]
            at = index("ctx")
            digit = (at >> low) & (radix - 1)
            earlier = [((digit ^ bits) < digit).astype(jnp.int32).astype(F32) for bits in range(1, radix)]
            total_before = sum(c[...].astype(F32) * e for c, e in zip(came, earlier))
            if not last:
                out_group, out_before = rest[-2:]
                if len(rest) == 3:
                    total_before = total_before + rest[0][...]
                out_before[...] = total_before
                out_group[...] = first[0][...] + first[1][...].astype(F32) + sum(c[...].astype(F32) for c in came)
                return
            out_theirs, out_ours = rest[-2:]
            own_ref, partner_ref = rest[:2] if len(rest) >= 4 else first
            if len(rest) > 2:
                total_before = total_before + rest[-3][...]
            odd = (at & 1).astype(F32)
            out_theirs[...] = (total_before + own_ref[...] * (1.0 - odd)).astype(BF16)
            out_ours[...] = (total_before + partner_ref[...].astype(F32) * odd).astype(BF16)

        start = [own, partner] if span == 1 else [group, jnp.zeros_like(partner)]
        extra = ([own, partner] if last and span > 1 else []) + before
        outs = [arr(H, H), arr(H, H)] if last else [arr(H, H, dtype=F32)] * 2
        result = call(combine_kernel, start + came + extra, outs, 0)
        if not last:
            group, before = result[0], [result[1]]
        span *= radix
    theirs, ours = result
    other = swap(theirs, "ctx", 1)

    def inner_kernel(own, r1, r2, r3, s, k, v0, v1, o_q, o_m):
        rows = lax.broadcasted_iota(jnp.int32, (steps, steps), 0)
        causal = rows >= lax.broadcasted_iota(jnp.int32, (steps, steps), 1)
        for h, v in enumerate((v0, v1)):
            at = slice(h * H, h * H + H)
            u = own[:, at] + r1[:, at].astype(F32) + r2[:, at].astype(F32) + r3[:, at].astype(F32)
            q = feature(u * s[...]).astype(BF16)
            o_q[:, at] = q
            sc = lax.dot_general(q, k[:, at], (((1,), (1,)), ((), ())), preferred_element_type=F32)
            sc = jnp.where(causal, sc, 0.0).astype(BF16)
            o_m[:, at] = mm(sc, v[...])

    outs = [arr(steps, width), arr(steps, width, dtype=F32)]
    queries, inner = call(inner_kernel, [own_q, *q_others, scale, keys, values_0, values_1], outs, 8 * steps * steps * H)

    def outer_kernel(q, inner, ours, other, hg, o):
        odd = (index("ctx") & 1) == 1
        a, b = ours[...].astype(F32), other[...].astype(F32)
        prior = jnp.where(odd, b, a).astype(BF16), jnp.where(odd, a, b).astype(BF16)
        for h in range(heads):
            at = slice(h * H, h * H + H)
            mixed = inner[:, at] + mm(q[:, at], prior[h])
            factor = lax.rsqrt(jnp.mean(mixed * mixed, axis=-1, keepdims=True) + epsilon)
            o[:, at] = (mixed * factor * hg[:, at]).astype(BF16)

    (out,) = call(outer_kernel, [queries, inner, ours, other, head_gain.reshape(1, width)], [arr(steps, width)], 4 * steps * H * H)
    return out


def solution(mesh):
    in_specs = (P("ctx", "dp"), P(), P(None, "dp", None), P("dp"))
    out_specs = P("ctx", "dp")

    return jax.shard_map(body, mesh=mesh, in_specs=in_specs, out_specs=out_specs, check_vma=False)
```

time: 43.8 us -> 48.1 us (1.098)
  waiting for transfers between devices: 14.1 us -> 20.6 us
  starting transfers between devices: 20.7 us -> 19.1 us
  Pallas kernels: 8.69 us -> 8.05 us
    ppermute x0 -> x6, waiting for transfers between devices: none -> 17 us  [swap_by_core(): return lax.ppermute(value, ('dp', 'ctx'), pairs)]
    ppermute x16 -> x6, starting transfers between devices: 20.7 us -> 8.72 us  [swap(): lax.ppermute(value, axis, [(i, i ^ bits) for i in range(lax.axis_size(axi...]
    ppermute x16 -> x6, waiting for transfers between devices: 14.1 us -> 3.52 us  [swap(): lax.ppermute(value, axis, [(i, i ^ bits) for i in range(lax.axis_size(axi...]
    ppermute x0 -> x6, starting transfers between devices: none -> 10.4 us  [swap_by_core(): return lax.ppermute(value, ('dp', 'ctx'), pairs)]
    pallas_call x11, Pallas kernels: 8.69 us -> 8.05 us  [call(): pl.pallas_call(kernel, in_specs=specs or [vmem] * len(arrays), out_specs=...]
  transfers between devices with their start and end apart: 16 -> 12, of which waited for: 7 -> 5; matrix products, arithmetic and copies ran while one was open for 0% -> 0% of each run, Pallas kernels for 11% -> 9%
where the time goes in v3:
time: 48.1 us; the launch traced here: 47.9 us
  waiting for transfers between devices  20.6 us (43%)
  starting transfers between devices  19.1 us (40%)
  Pallas kernels  8.05 us (17%)
    ppermute x6, waiting for transfers between devices, swap_by_core(): return lax.ppermute(value, ('dp', 'ctx'), pairs)  17 us
    ppermute x6, starting transfers between devices, swap_by_core(): return lax.ppermute(value, ('dp', 'ctx'), pairs)  10.4 us
    ppermute x6, starting transfers between devices, swap(): lax.ppermute(value, axis, [(i, i ^ bits) for i in range(lax.axis_size(axi...  8.72 us
    pallas_call x11, Pallas kernels, call(): pl.pallas_call(kernel, in_specs=specs or [vmem] * len(arrays), out_specs=...  8.05 us
    ppermute x6, waiting for transfers between devices, swap(): lax.ppermute(value, axis, [(i, i ^ bits) for i in range(lax.axis_size(axi...  3.52 us
  transfers between devices with their start and end apart: 12, of which 5 were waited for; matrix products, arithmetic and copies ran while one was open for 0% of the time, Pallas kernels for 9%

profile of v3, /device:TPU:0, one launch (start us, length us, event | category | flops | bytes accessed | tf_op | source)
XLA Modules:
  0.0 47.9 jit_solution(16784805480308310285)
XLA Ops:
  0.0 2.5 %shard_map.46 = (bf16[528,768]{1,0:T(8,128)(2,1)S(1)}, bf16[512,512]{1,0:T(8,128)(2,1)S(1)}, bf16[512,1024]{1,0:T(8,128)(2,1)S(1)}, bf16[512,1024]{1,0:T(8,128)(2,1)S(1)}, f32[16,512]{1,0:T(8,128)S(1)}) custom-call(bf16[512,512]{1,0:T(8,128)(2,1)} %x_hbm.1, f32[1,2048]{1,0:T(1,128)} %bitcast.3, bf16[3,512,1024]{2,1,0:T(8,128)(2,1)} %w_hbm.3), custom_call_target="tpu_custom_call" | custom-call | flops 402653184 | bytes 7143424 | tf_op jit(solution)/shard_map/pallas_call | solution.py:64
  2.5 3.0 %collective-permute-start.3 = (bf16[528,768]{1,0:T(8,128)(2,1)S(1)}, bf16[528,768]{1,0:T(8,128)(2,1)S(1)}, u32[]{:S(2)}, u32[]{:S(2)}) collective-permute-start(bf16[528,768]{1,0:T(8,128)(2,1)S(1)} %get-tuple-element.41), channel_id=1, source_target_pairs={{0,8},{1,17},{2,10},{3,19},{4,12},{5,21},{6,14},{7,23},{8,0},{9,25... | collective-permute-start | bytes 2433032 | tf_op jit(solution)/shard_map/ppermute | solution.py:36
  5.6 0.4 shard_map.49
  6.0 9.8 %collective-permute-done.3.r.a = bf16[528,768]{1,0:T(8,128)(2,1)S(1)} collective-permute-done((bf16[528,768]{1,0:T(8,128)(2,1)S(1)}, bf16[528,768]{1,0:T(8,128)(2,1)S(1)}, u32[]{:S(2)}, u32[]{:S(2)}) %collective-permute-start.3) | collective-permute-done | bytes 811040 | tf_op jit(solution)/shard_map/ppermute | solution.py:36
  15.8 0.1 shard_map.50
  15.9 2.1 %collective-permute-start.4 = (bf16[528,384]{1,0:T(8,128)(2,1)S(1)}, bf16[528,384]{1,0:T(8,128)(2,1)S(1)}, u32[]{:S(2)}, u32[]{:S(2)}) collective-permute-start(bf16[528,384]{1,0:T(8,128)(2,1)S(1)} %shard_map.50), channel_id=1, source_target_pairs={{0,16},{1,9},{2,18},{3,11},{4,20},{5,13},{6,22},{7,15},{8,24},{9,1... | collective-permute-start | bytes 1216520 | tf_op jit(solution)/shard_map/ppermute | solution.py:36
  18.0 1.2 %shard_map.47 = (bf16[512,256]{1,0:T(8,128)(2,1)S(1)}, bf16[512,1024]{1,0:T(8,128)(2,1)S(1)}) custom-call(bf16[512,512]{1,0:T(8,128)(2,1)S(1)} %get-tuple-element.31.x, bf16[512,1024]{1,0:T(8,128)(2,1)S(1)} %get-tuple-element.33.wv, bf16[3,512,1024]{2,1,0:T(8,128)(2,1)} %w_hbm.3), custom_call_target="tpu_custom_call" | custom-call | flops 134217728 | bytes 6029312 | tf_op jit(solution)/shard_map/pallas_call | solution.py:64
  19.3 1.6 %collective-permute-start.5 = (bf16[512,256]{1,0:T(8,128)(2,1)S(1)}, bf16[512,256]{1,0:T(8,128)(2,1)S(1)}, u32[]{:S(2)}, u32[]{:S(2)}) collective-permute-start(bf16[512,256]{1,0:T(8,128)(2,1)S(1)} %get-tuple-element.47), channel_id=1, source_target_pairs={{0,8},{1,17},{2,10},{3,19},{4,12},{5,21},{6,14},{7,23},{8,0},{9,25... | collective-permute-start | bytes 786440 | tf_op jit(solution)/shard_map/ppermute | solution.py:36
  20.8 4.9 %collective-permute-done.5.r.a = bf16[512,256]{1,0:T(8,128)(2,1)S(1)} collective-permute-done((bf16[512,256]{1,0:T(8,128)(2,1)S(1)}, bf16[512,256]{1,0:T(8,128)(2,1)S(1)}, u32[]{:S(2)}, u32[]{:S(2)}) %collective-permute-start.5) | collective-permute-done | bytes 262176 | tf_op jit(solution)/shard_map/ppermute | solution.py:36
  25.7 1.1 %collective-permute-start.6 = (bf16[512,128]{1,0:T(8,128)(2,1)S(1)}, bf16[512,128]{1,0:T(8,128)(2,1)S(1)}, u32[]{:S(2)}, u32[]{:S(2)}) collective-permute-start(bf16[512,128]{1,0:T(8,128)(2,1)S(1)} %shard_map.52), channel_id=1, source_target_pairs={{0,16},{1,9},{2,18},{3,11},{4,20},{5,13},{6,22},{7,15},{8,24},{9,1... | collective-permute-start | bytes 393224 | tf_op jit(solution)/shard_map/ppermute | solution.py:36
  26.9 1.0 %shard_map.48 = (f32[512,256]{1,0:T(8,128)S(1)}, f32[512,256]{1,0:T(8,128)S(1)}, f32[512,256]{1,0:T(8,128)S(1)}, bf16[512,256]{1,0:T(8,128)(2,1)S(1)}, bf16[512,...) custom-call(bf16[512,512]{1,0:T(8,128)(2,1)S(1)} %get-tuple-element.31.x, bf16[512,1024]{1,0:T(8,128)(2,1)S(1)} %get-tuple-element.32.wk, ...), custom_call_target="tpu_custom_call" | custom-call | flops 805306368 | bytes 6029312 | tf_op jit(solution)/shard_map/pallas_call | solution.py:64
  27.8 0.0 copy-start
  27.9 0.0 collective-permute-done.4.b
  27.9 0.5 %shard_map.51 = (bf16[512,256]{1,0:T(8,128)(2,1)S(1)}, bf16[512,128]{1,0:T(8,128)(2,1)S(1)}, f32[512,128]{1,0:T(8,128)S(1)}, f32[128,128]{1,0:T(8,128)S(1)}) custom-call(f32[512,256]{1,0:T(8,128)S(1)} %get-tuple-element.39.own_k, f32[512,256]{1,0:T(8,128)S(1)} %get-tuple-element.40.own_v.own, bf16[528,768]{1,0:T(8,128)(2,1)S(1)} %collective-permute-done.3.r.a, ...), custom_call_target="tpu_custom_call" | custom-call | flops 16777216 | bytes 3018752 | tf_op jit(solution)/shard_map/pallas_call | solution.py:64
  28.4 2.4 %collective-permute-done.6.b = bf16[512,128]{1,0:T(8,128)(2,1)S(1)} collective-permute-done((bf16[512,128]{1,0:T(8,128)(2,1)S(1)}, bf16[512,128]{1,0:T(8,128)(2,1)S(1)}, u32[]{:S(2)}, u32[]{:S(2)}) %collective-permute-start.6) | collective-permute-done | bytes 131104 | tf_op jit(solution)/shard_map/ppermute | solution.py:36
  30.8 0.2 shard_map.53
  31.0 0.1 collective-permute-start.7
  31.1 1.1 %collective-permute-start = (bf16[512,256]{1,0:T(8,128)(2,1)S(1)}, bf16[512,256]{1,0:T(8,128)(2,1)S(1)}, u32[]{:S(2)}, u32[]{:S(2)}) collective-permute-start(bf16[512,256]{1,0:T(8,128)(2,1)S(1)} %get-tuple-element.36), channel_id=1, source_target_pairs={{0,16},{1,9},{2,18},{3,11},{4,20},{5,13},{6,22},{7,15},{8,24},{9,1... | collective-permute-start | bytes 786440 | tf_op jit(solution)/shard_map/ppermute | solution.py:36
  32.2 1.5 %collective-permute-start.1 = (bf16[512,256]{1,0:T(8,128)(2,1)S(1)}, bf16[512,256]{1,0:T(8,128)(2,1)S(1)}, u32[]{:S(2)}, u32[]{:S(2)}) collective-permute-start(bf16[512,256]{1,0:T(8,128)(2,1)S(1)} %get-tuple-element.37), channel_id=1, source_target_pairs={{0,8},{1,17},{2,10},{3,19},{4,12},{5,21},{6,14},{7,23},{8,0},{9,25... | collective-permute-start | bytes 786440 | tf_op jit(solution)/shard_map/ppermute | solution.py:36
  33.7 1.0 %collective-permute-start.2 = (bf16[512,256]{1,0:T(8,128)(2,1)S(1)}, bf16[512,256]{1,0:T(8,128)(2,1)S(1)}, u32[]{:S(2)}, u32[]{:S(2)}) collective-permute-start(bf16[512,256]{1,0:T(8,128)(2,1)S(1)} %get-tuple-element.38), channel_id=1, source_target_pairs={{0,24},{8,16},{16,8},{24,0},{1,25},{9,17},{17,9},{25,1},{2,26},{10... | collective-permute-start | bytes 786440 | tf_op jit(solution)/shard_map/ppermute | solution.py:26
  34.7 0.0 collective-permute-done.7.refs_1_
  34.7 1.6 %collective-permute-start.8 = (bf16[128,128]{1,0:T(8,128)(2,1)S(1)}, bf16[128,128]{1,0:T(8,128)(2,1)S(1)}, u32[]{:S(2)}, u32[]{:S(2)}) collective-permute-start(bf16[128,128]{1,0:T(8,128)(2,1)S(1)} %add_convert_fusion), channel_id=1, source_target_pairs={{0,2},{1,3},{2,0},{3,1},{4,6},{5,7},{6,4},{7,5},{8,10},{9,11},{10,... | collective-permute-start | bytes 98312 | tf_op jit(solution)/shard_map/ppermute | solution.py:26
  36.3 2.6 %collective-permute-start.9 = (bf16[128,128]{1,0:T(8,128)(2,1)S(1)}, bf16[128,128]{1,0:T(8,128)(2,1)S(1)}, u32[]{:S(2)}, u32[]{:S(2)}) collective-permute-start(bf16[128,128]{1,0:T(8,128)(2,1)S(1)} %add_convert_fusion), channel_id=1, source_target_pairs={{0,4},{1,5},{2,6},{3,7},{4,0},{5,1},{6,2},{7,3},{8,12},{9,13},{10,... | collective-permute-start | bytes 98312 | tf_op jit(solution)/shard_map/ppermute | solution.py:26
  38.9 0.0 collective-permute-done.8.refs_2_
  38.9 3.4 %collective-permute-start.10 = (bf16[128,128]{1,0:T(8,128)(2,1)S(1)}, bf16[128,128]{1,0:T(8,128)(2,1)S(1)}, u32[]{:S(2)}, u32[]{:S(2)}) collective-permute-start(bf16[128,128]{1,0:T(8,128)(2,1)S(1)} %add_convert_fusion), channel_id=1, source_target_pairs={{0,6},{1,7},{2,4},{3,5},{4,2},{5,3},{6,0},{7,1},{8,14},{9,15},{10,... | collective-permute-start | bytes 98312 | tf_op jit(solution)/shard_map/ppermute | solution.py:26
  42.3 0.0 collective-permute-done.9.refs_3_
  42.3 2.3 %collective-permute-done.10.refs_4_ = bf16[128,128]{1,0:T(8,128)(2,1)S(1)} collective-permute-done((bf16[128,128]{1,0:T(8,128)(2,1)S(1)}, bf16[128,128]{1,0:T(8,128)(2,1)S(1)}, u32[]{:S(2)}, u32[]{:S(2)}) %collective-permute-start.10) | collective-permute-done | bytes 32800 | tf_op jit(solution)/shard_map/ppermute | solution.py:26
  44.7 0.1 collective-permute-start.11
  44.7 0.0 collective-permute-done.r1
  44.8 0.0 collective-permute-done.1.r2
  44.8 1.2 %collective-permute-done.2.r3 = bf16[512,256]{1,0:T(8,128)(2,1)S(1)} collective-permute-done((bf16[512,256]{1,0:T(8,128)(2,1)S(1)}, bf16[512,256]{1,0:T(8,128)(2,1)S(1)}, u32[]{:S(2)}, u32[]{:S(2)}) %collective-permute-start.2) | collective-permute-done | bytes 262176 | tf_op jit(solution)/shard_map/ppermute | solution.py:26
  46.0 0.8 %shard_map.54 = (bf16[512,256]{1,0:T(8,128)(2,1)S(1)}, f32[512,256]{1,0:T(8,128)S(1)}) custom-call(f32[512,256]{1,0:T(8,128)S(1)} %get-tuple-element.35.own, bf16[512,256]{1,0:T(8,128)(2,1)S(1)} %collective-permute-done.r1, bf16[512,256]{1,0:T(8,128)(2,1)S(1)} %collective-permute-done.1.r2, bf16[512,256]{1,0:T(8,128)(2,1)S(1)} %collective-permute-done.2.r3, ...), custom_call_target="tpu_custom_call" | custom-call | flops 268435456 | bytes 2883584 | tf_op jit(solution)/shard_map/pallas_call | solution.py:64
  46.8 0.0 collective-permute-done.11.other
  46.8 0.0 copy-done
  46.8 1.1 %shard_map.56 = bf16[512,256]{1,0:T(8,128)(2,1)} custom-call(bf16[512,256]{1,0:T(8,128)(2,1)S(1)} %get-tuple-element.51.q, f32[512,256]{1,0:T(8,128)S(1)} %get-tuple-element.52.inner, bf16[128,128]{1,0:T(8,128)(2,1)S(1)} %get-tuple-element.55.ours, bf16[128,128]{1,0:T(8,128)(2,1)S(1)} %collective-permute-done.11.other, f32[1,256]{1,0:T(1,128)S(1)} %bitcast.2), custom_call_target="tpu_custom_call" | custom-call | flops 33554432 | bytes 1115136 | tf_op jit(solution)/shard_map/pallas_call | solution.py:64
  (3 shorter events, 0.1 us)
Async XLA Ops:
  2.5 13.3 %collective-permute-start.3 = (bf16[528,768]{1,0:T(8,128)(2,1)S(1)}, bf16[528,768]{1,0:T(8,128)(2,1)S(1)}, u32[]{:S(2)}, u32[]{:S(2)}) collective-permute-start(bf16[528,768]{1,0:T(8,128)(2,1)S(1)} %get-tuple-element.41), channel_id=1, source_target_pairs={{0,8},{1,17},{2,10},{3,19},{4,12},{5,21},{6,14},{7,23},{8,0},{9,25... | collective-permute-start | bytes 2433032 | tf_op jit(solution)/shard_map/ppermute | solution.py:36
  15.9 12.0 %collective-permute-start.4 = (bf16[528,384]{1,0:T(8,128)(2,1)S(1)}, bf16[528,384]{1,0:T(8,128)(2,1)S(1)}, u32[]{:S(2)}, u32[]{:S(2)}) collective-permute-start(bf16[528,384]{1,0:T(8,128)(2,1)S(1)} %shard_map.50), channel_id=1, source_target_pairs={{0,16},{1,9},{2,18},{3,11},{4,20},{5,13},{6,22},{7,15},{8,24},{9,1... | collective-permute-start | bytes 1216520 | tf_op jit(solution)/shard_map/ppermute | solution.py:36
  19.3 6.4 %collective-permute-start.5 = (bf16[512,256]{1,0:T(8,128)(2,1)S(1)}, bf16[512,256]{1,0:T(8,128)(2,1)S(1)}, u32[]{:S(2)}, u32[]{:S(2)}) collective-permute-start(bf16[512,256]{1,0:T(8,128)(2,1)S(1)} %get-tuple-element.47), channel_id=1, source_target_pairs={{0,8},{1,17},{2,10},{3,19},{4,12},{5,21},{6,14},{7,23},{8,0},{9,25... | collective-permute-start | bytes 786440 | tf_op jit(solution)/shard_map/ppermute | solution.py:36
  25.7 5.0 %collective-permute-start.6 = (bf16[512,128]{1,0:T(8,128)(2,1)S(1)}, bf16[512,128]{1,0:T(8,128)(2,1)S(1)}, u32[]{:S(2)}, u32[]{:S(2)}) collective-permute-start(bf16[512,128]{1,0:T(8,128)(2,1)S(1)} %shard_map.52), channel_id=1, source_target_pairs={{0,16},{1,9},{2,18},{3,11},{4,20},{5,13},{6,22},{7,15},{8,24},{9,1... | collective-permute-start | bytes 393224 | tf_op jit(solution)/shard_map/ppermute | solution.py:36
  27.8 19.0 %copy-start = (f32[256]{0:T(256)S(1)}, f32[256]{0:T(256)}, u32[]{:S(2)}) copy-start(f32[256]{0:T(256)} %param.7) | copy-start | bytes 3076
  31.0 3.6 %collective-permute-start.7 = (bf16[128,128]{1,0:T(8,128)(2,1)S(1)}, bf16[128,128]{1,0:T(8,128)(2,1)S(1)}, u32[]{:S(2)}, u32[]{:S(2)}) collective-permute-start(bf16[128,128]{1,0:T(8,128)(2,1)S(1)} %get-tuple-element.54), channel_id=1, source_target_pairs={{0,1},{1,0},{2,3},{3,2},{4,5},{5,4},{6,7},{7,6},{8,9},{9,8},{10,11... | collective-permute-start | bytes 98312 | tf_op jit(solution)/shard_map/ppermute | solution.py:26
  31.1 13.6 %collective-permute-start = (bf16[512,256]{1,0:T(8,128)(2,1)S(1)}, bf16[512,256]{1,0:T(8,128)(2,1)S(1)}, u32[]{:S(2)}, u32[]{:S(2)}) collective-permute-start(bf16[512,256]{1,0:T(8,128)(2,1)S(1)} %get-tuple-element.36), channel_id=1, source_target_pairs={{0,16},{1,9},{2,18},{3,11},{4,20},{5,13},{6,22},{7,15},{8,24},{9,1... | collective-permute-start | bytes 786440 | tf_op jit(solution)/shard_map/ppermute | solution.py:36
  32.2 12.5 %collective-permute-start.1 = (bf16[512,256]{1,0:T(8,128)(2,1)S(1)}, bf16[512,256]{1,0:T(8,128)(2,1)S(1)}, u32[]{:S(2)}, u32[]{:S(2)}) collective-permute-start(bf16[512,256]{1,0:T(8,128)(2,1)S(1)} %get-tuple-element.37), channel_id=1, source_target_pairs={{0,8},{1,17},{2,10},{3,19},{4,12},{5,21},{6,14},{7,23},{8,0},{9,25... | collective-permute-start | bytes 786440 | tf_op jit(solution)/shard_map/ppermute | solution.py:36
  33.7 12.3 %collective-permute-start.2 = (bf16[512,256]{1,0:T(8,128)(2,1)S(1)}, bf16[512,256]{1,0:T(8,128)(2,1)S(1)}, u32[]{:S(2)}, u32[]{:S(2)}) collective-permute-start(bf16[512,256]{1,0:T(8,128)(2,1)S(1)} %get-tuple-element.38), channel_id=1, source_target_pairs={{0,24},{8,16},{16,8},{24,0},{1,25},{9,17},{17,9},{25,1},{2,26},{10... | collective-permute-start | bytes 786440 | tf_op jit(solution)/shard_map/ppermute | solution.py:26
  34.7 4.2 %collective-permute-start.8 = (bf16[128,128]{1,0:T(8,128)(2,1)S(1)}, bf16[128,128]{1,0:T(8,128)(2,1)S(1)}, u32[]{:S(2)}, u32[]{:S(2)}) collective-permute-start(bf16[128,128]{1,0:T(8,128)(2,1)S(1)} %add_convert_fusion), channel_id=1, source_target_pairs={{0,2},{1,3},{2,0},{3,1},{4,6},{5,7},{6,4},{7,5},{8,10},{9,11},{10,... | collective-permute-start | bytes 98312 | tf_op jit(solution)/shard_map/ppermute | solution.py:26
  36.3 6.0 %collective-permute-start.9 = (bf16[128,128]{1,0:T(8,128)(2,1)S(1)}, bf16[128,128]{1,0:T(8,128)(2,1)S(1)}, u32[]{:S(2)}, u32[]{:S(2)}) collective-permute-start(bf16[128,128]{1,0:T(8,128)(2,1)S(1)} %add_convert_fusion), channel_id=1, source_target_pairs={{0,4},{1,5},{2,6},{3,7},{4,0},{5,1},{6,2},{7,3},{8,12},{9,13},{10,... | collective-permute-start | bytes 98312 | tf_op jit(solution)/shard_map/ppermute | solution.py:26
  38.9 5.7 %collective-permute-start.10 = (bf16[128,128]{1,0:T(8,128)(2,1)S(1)}, bf16[128,128]{1,0:T(8,128)(2,1)S(1)}, u32[]{:S(2)}, u32[]{:S(2)}) collective-permute-start(bf16[128,128]{1,0:T(8,128)(2,1)S(1)} %add_convert_fusion), channel_id=1, source_target_pairs={{0,6},{1,7},{2,4},{3,5},{4,2},{5,3},{6,0},{7,1},{8,14},{9,15},{10,... | collective-permute-start | bytes 98312 | tf_op jit(solution)/shard_map/ppermute | solution.py:26
  44.7 2.1 %collective-permute-start.11 = (bf16[128,128]{1,0:T(8,128)(2,1)S(1)}, bf16[128,128]{1,0:T(8,128)(2,1)S(1)}, u32[]{:S(2)}, u32[]{:S(2)}) collective-permute-start(bf16[128,128]{1,0:T(8,128)(2,1)S(1)} %get-tuple-element.56), channel_id=1, source_target_pairs={{0,1},{1,0},{2,3},{3,2},{4,5},{5,4},{6,7},{7,6},{8,9},{9,8},{10,11... | collective-permute-start | bytes 98312 | tf_op jit(solution)/shard_map/ppermute | solution.py:26

commit v4 on v3

--- a/solution.py
+++ b/solution.py
@@ -79,9 +79,6 @@
     def cols(bits):
         return pl.ds(pl.multiple_of((index("dp") ^ bits) * width, width), width)
 
-    def head_cols(bits, head):
-        return pl.ds(pl.multiple_of((index("dp") ^ bits) * width + head * H, H), H)
-
     def squares(xf):
         sq = xf * xf
         hi = sq.astype(BF16)
@@ -110,51 +107,50 @@
 
     C = width + H
 
-    def first_1_kernel(x_hbm, gain_hbm, w_hbm, o, o_xg, o_wk, o_wv, o_sq, x, gain, sem):
-        a = first_hop()
+    def first_k_kernel(x_hbm, gain_hbm, w_hbm, o, o_xg, x, gain, w, sem):
         copies = [pltpu.make_async_copy(x_hbm, x, sem.at[0]), pltpu.make_async_copy(gain_hbm, gain, sem.at[1])]
-        for i, bits in enumerate((a, 3, 3 - a, 0)):
-            at = cols(bits)
-            copies.append(pltpu.make_async_copy(w_hbm.at[K, :, at], o_wk.at[:, at], sem.at[2 + 2 * i]))
-            copies.append(pltpu.make_async_copy(w_hbm.at[V, :, at], o_wv.at[:, at], sem.at[3 + 2 * i]))
+        for i, bits in enumerate((first_hop(), 3)):
+            copies.append(pltpu.make_async_copy(w_hbm.at[K, :, cols(bits)], w.at[i], sem.at[2 + i]))
         for c in copies:
             c.start()
         copies[0].wait()
         copies[1].wait()
-        xf = x[...].astype(F32)
         g = gain[:, pl.ds(pl.multiple_of(index("dp") * features, features), features)]
-        xg = (xf * g).astype(BF16)
+        xg = (x[...].astype(F32) * g).astype(BF16)
         o_xg[...] = xg
-        ss = squares(xf)
+        for i in range(2):
+            copies[2 + i].wait()
+            o[:, i * width:i * width + width] = mm(xg, w[i]).astype(BF16)
+
+    outs = [arr(steps, 2 * width), arr(steps, features)]
+    scratch = [pltpu.VMEM((steps, features), BF16), pltpu.VMEM((1, total), F32), pltpu.VMEM((2, features, width), BF16), pltpu.SemaphoreType.DMA((4,))]
+    in_hbm = [pltpu.with_memory_space_constraint(a, pltpu.HBM) for a in (tokens, input_gain.reshape(1, total), projections)]
+    s0, xg = call(first_k_kernel, in_hbm, outs, 4 * block, [hbm] * 3, scratch)
+    ka1 = swap_by_core(s0, 1, 2)
+
+    def first_v_kernel(xg_ref, x_hbm, w_hbm, o0, o1, o_wk, o_wv, o_wq, o_sq, x, sem):
+        copies = [pltpu.make_async_copy(x_hbm, x, sem.at[3])]
+        copies += [pltpu.make_async_copy(w_hbm.at[p], o, sem.at[i]) for i, (p, o) in enumerate(((V, o_wv), (K, o_wk), (Q, o_wq)))]
+        for c in copies:
+            c.start()
+        copies[0].wait()
+        ss = squares(x[...].astype(F32))
         o_sq[...] = ss
-        o[steps:, :2 * width] = sum_rows(ss, 2 * width)
-        o[steps:, 2 * width:] = jnp.zeros((R, 2 * C - 2 * width), BF16)
-        for i, bits in enumerate((a, 3)):
-            copies[2 + 2 * i].wait()
-            copies[3 + 2 * i].wait()
-            at = i * C
-            o[:steps, at:at + width] = mm(xg, o_wk[:, cols(bits)]).astype(BF16)
-            o[:steps, at + width:at + C] = mm(xg, o_wv[:, head_cols(bits, 0)]).astype(BF16)
-        for c in copies[6:]:
-            c.wait()
-
-    outs = [arr(steps + R, 2 * C), arr(steps, features), arr(features, columns), arr(features, columns), arr(R, steps, dtype=F32)]
-    scratch = [pltpu.VMEM((steps, features), BF16), pltpu.VMEM((1, total), F32), pltpu.SemaphoreType.DMA((10,))]
-    in_hbm = [pltpu.with_memory_space_constraint(a, pltpu.HBM) for a in (tokens, input_gain.reshape(1, total), projections)]
-    s0, xg, w_k, w_v, sq = call(first_1_kernel, in_hbm, outs, 6 * block, [hbm] * 3, scratch)
-    a1 = swap_by_core(s0, 1, 2)
-
-    def first_2_kernel(x, wv, w_hbm, o, o_wq, sem):
-        cq = pltpu.make_async_copy(w_hbm.at[Q], o_wq, sem.at[0])
-        cq.start()
-        xg = x[...]
-        o[:, :H] = mm(xg, wv[:, head_cols(first_hop(), 1)]).astype(BF16)
-        o[:, H:] = mm(xg, wv[:, head_cols(3, 1)]).astype(BF16)
-        cq.wait()
-
-    outs = [arr(steps, 2 * H), arr(features, columns)]
-    s0, w_q = call(first_2_kernel, [xg, w_v, in_hbm[2]], outs, 2 * block, [vmem, vmem, hbm], [pltpu.SemaphoreType.DMA((1,))])
-    b1 = swap_by_core(s0, 1, 2)
+        o0[steps:, :] = sum_rows(ss, 2 * H)
+        copies[1].wait()
+        xg = xg_ref[...]
+        for i, bits in enumerate((first_hop(), 3)):
+            v = mm(xg, o_wv[:, cols(bits)]).astype(BF16)
+            o0[:steps, i * H:i * H + H] = v[:, :H]
+            o1[:, i * H:i * H + H] = v[:, H:]
+        copies[2].wait()
+        copies[3].wait()
+
+    outs = [arr(steps + R, 2 * H), arr(steps, 2 * H)] + [arr(features, columns)] * 3 + [arr(R, steps, dtype=F32)]
+    scratch = [pltpu.VMEM((steps, features), BF16), pltpu.SemaphoreType.DMA((4,))]
+    s0, s1, w_k, w_v, w_q, sq = call(first_v_kernel, [xg, in_hbm[0], in_hbm[2]], outs, 4 * block, [vmem, hbm, hbm], scratch)
+    va1 = swap_by_core(s0, 1, 2)
+    b1 = swap_by_core(s1, 1, 2)
 
     def onward_kernel(x, wk, wv, pass_a, pass_b):
         xg = x[...]
@@ -177,12 +173,13 @@
     outs = [arr(steps, width, dtype=F32)] * 3 + [arr(steps, width)] * 3
     own_k, own_v, own_q, *sends = call(rest_kernel, [xg, w_k, w_v, w_q], outs, 12 * block)
 
-    def second_1_kernel(p, r, sq, o):
-        o[:steps, :] = (p[...] + r[:steps, C:].astype(F32)).astype(BF16)
-        o[steps:, :width] = sum_rows(sq[...] + read_rows(r[steps:, :2 * width], 2 * width), width)
+    def second_1_kernel(p, r, rv, sq, o):
+        o[:steps, :width] = (p[:, :width] + r[:, width:].astype(F32)).astype(BF16)
+        o[:steps, width:] = (p[:, width:] + rv[:steps, H:].astype(F32)).astype(BF16)
+        o[steps:, :width] = sum_rows(sq[...] + read_rows(rv[steps:, :], 2 * H), width)
         o[steps:, width:] = jnp.zeros((R, H), BF16)
 
-    (s0,) = call(second_1_kernel, [pass_a, a1, sq], [arr(steps + R, C)], 0)
+    (s0,) = call(second_1_kernel, [pass_a, ka1, va1, sq], [arr(steps + R, C)], 0)
     a2 = swap_by_core(s0, 2, 1)
 
     def second_2_kernel(p, r, o):
@@ -195,22 +192,21 @@
     def state_of(k, v):
         return lax.dot_general(k, v, (((0,), (0,)), ((), ())), preferred_element_type=F32)
 
-    def keys_kernel(own_k, own_v, a, b, sq, o_k, o_v, o_s, o_st):
-        ss = sq[:1, :] + read_rows(a[steps:, :2 * width], 2 * width) + read_rows(b[steps:, :width], width)
+    def keys_kernel(own_k, own_v, a, va, b, sq, o_k, o_v, o_s, o_st):
+        ss = sq[:1, :] + read_rows(va[steps:, :], 2 * H) + read_rows(b[steps:, :width], width)
         inv = lax.rsqrt(ss * (1.0 / total) + epsilon)
         scale = jnp.broadcast_to(inv, (H, steps)).T
         o_s[...] = scale
         for h in range(heads):
             at = slice(h * H, h * H + H)
-            u = (own_k[:, at] + a[:steps, at].astype(F32) + b[:steps, at].astype(F32)) * scale
+            u = (own_k[:, at] + a[:, at].astype(F32) + b[:steps, at].astype(F32)) * scale
             o_k[:, at] = feature(u).astype(BF16)
-        at = slice(width, C)
-        val = ((own_v[:, :H] + a[:steps, at].astype(F32) + b[:steps, at].astype(F32)) * scale).astype(BF16)
+        val = ((own_v[:, :H] + va[:steps, :H].astype(F32) + b[:steps, width:].astype(F32)) * scale).astype(BF16)
         o_v[...] = val
         o_st[...] = state_of(o_k[:, :H], val)
 
     outs = [arr(steps, width), arr(steps, H), arr(steps, H, dtype=F32), arr(H, H, dtype=F32)]
-    keys, values_0, scale, state_0 = call(keys_kernel, [own_k, own_v, a1, a2, sq], outs, 2 * steps * H * H)
+    keys, values_0, scale, state_0 = call(keys_kernel, [own_k, own_v, ka1, va1, a2, sq], outs, 2 * steps * H * H)
 
     def values_kernel(k, own, a, b, s, st0, o_v, o_own, o_give):
         val = ((own[:, H:] + a[:, :H].astype(F32) + b[...].astype(F32)) * s[...]).astype(BF16)

time: 48.1 us -> 47.3 us (0.983)
  waiting for transfers between devices: 20.6 us -> 18.6 us
  starting transfers between devices: 19.1 us -> 20.1 us
    ppermute x6 -> x7, waiting for transfers between devices: 17 us -> 14.6 us  [swap_by_core(): return lax.ppermute(value, ('dp', 'ctx'), pairs)]
    ppermute x6 -> x7, starting transfers between devices: 10.4 us -> 11.8 us  [swap_by_core(): return lax.ppermute(value, ('dp', 'ctx'), pairs)]
    ppermute x6, starting transfers between devices: 8.72 us -> 8.24 us  [swap(): lax.ppermute(value, axis, [(i, i ^ bits) for i in range(lax.axis_size(axi...]
  transfers between devices with their start and end apart: 12 -> 13, of which waited for: 5 -> 5; matrix products, arithmetic and copies ran while one was open for 0% -> 0% of each run, Pallas kernels for 9% -> 10%
where the time goes in v4:
time: 47.3 us; the launch traced here: 47.1 us
  starting transfers between devices  20.1 us (42%)
  waiting for transfers between devices  18.6 us (39%)
  Pallas kernels  8.35 us (18%)
    ppermute x7, waiting for transfers between devices, swap_by_core(): return lax.ppermute(value, ('dp', 'ctx'), pairs)  14.6 us
    ppermute x7, starting transfers between devices, swap_by_core(): return lax.ppermute(value, ('dp', 'ctx'), pairs)  11.8 us
    pallas_call x11, Pallas kernels, call(): pl.pallas_call(kernel, in_specs=specs or [vmem] * len(arrays), out_specs=...  8.35 us
    ppermute x6, starting transfers between devices, swap(): lax.ppermute(value, axis, [(i, i ^ bits) for i in range(lax.axis_size(axi...  8.24 us
    ppermute x6, waiting for transfers between devices, swap(): lax.ppermute(value, axis, [(i, i ^ bits) for i in range(lax.axis_size(axi...  3.95 us
  transfers between devices with their start and end apart: 13, of which 5 were waited for; matrix products, arithmetic and copies ran while one was open for 0% of the time, Pallas kernels for 10%

profile of v4, /device:TPU:0, one launch (start us, length us, event | category | flops | bytes accessed | tf_op | source)
XLA Modules:
  0.0 47.1 jit_solution(20982703937207772)
XLA Ops:
  0.0 2.0 %shard_map.46 = (bf16[512,512]{1,0:T(8,128)(2,1)S(1)}, bf16[512,512]{1,0:T(8,128)(2,1)S(1)}) custom-call(bf16[512,512]{1,0:T(8,128)(2,1)} %x_hbm.3, f32[1,2048]{1,0:T(1,128)} %bitcast.3, bf16[3,512,1024]{2,1,0:T(8,128)(2,1)} %w_hbm.3), custom_call_target="tpu_custom_call" | custom-call | flops 268435456 | bytes 4726784 | tf_op jit(solution)/shard_map/pallas_call | solution.py:64
  2.0 3.0 %collective-permute-start.3 = (bf16[512,512]{1,0:T(8,128)(2,1)S(1)}, bf16[512,512]{1,0:T(8,128)(2,1)S(1)}, u32[]{:S(2)}, u32[]{:S(2)}) collective-permute-start(bf16[512,512]{1,0:T(8,128)(2,1)S(1)} %get-tuple-element.42), channel_id=1, source_target_pairs={{0,8},{1,17},{2,10},{3,19},{4,12},{5,21},{6,14},{7,23},{8,0},{9,25... | collective-permute-start | bytes 1572872 | tf_op jit(solution)/shard_map/ppermute | solution.py:36
  5.1 2.1 %shard_map.47 = (bf16[528,256]{1,0:T(8,128)(2,1)S(1)}, bf16[512,256]{1,0:T(8,128)(2,1)S(1)}, bf16[512,1024]{1,0:T(8,128)(2,1)S(1)}, bf16[512,1024]{1,0:T(8,128)(...) custom-call(bf16[512,512]{1,0:T(8,128)(2,1)S(1)} %get-tuple-element.32.xg_ref.x, bf16[512,512]{1,0:T(8,128)(2,1)} %x_hbm.3, ...), custom_call_target="tpu_custom_call" | custom-call | flops 268435456 | bytes 7905280 | tf_op jit(solution)/shard_map/pallas_call | solution.py:64
  7.1 0.1 collective-permute-start.4
  7.2 0.5 shard_map.49
  7.7 7.5 %collective-permute-done.4.rv.va = bf16[528,256]{1,0:T(8,128)(2,1)S(1)} collective-permute-done((bf16[528,256]{1,0:T(8,128)(2,1)S(1)}, bf16[528,256]{1,0:T(8,128)(2,1)S(1)}, u32[]{:S(2)}, u32[]{:S(2)}) %collective-permute-start.4) | collective-permute-done | bytes 270368 | tf_op jit(solution)/shard_map/ppermute | solution.py:36
  15.1 0.0 collective-permute-done.3.r.a
  15.1 0.1 shard_map.50
  15.2 2.1 %collective-permute-start.5 = (bf16[528,384]{1,0:T(8,128)(2,1)S(1)}, bf16[528,384]{1,0:T(8,128)(2,1)S(1)}, u32[]{:S(2)}, u32[]{:S(2)}) collective-permute-start(bf16[528,384]{1,0:T(8,128)(2,1)S(1)} %shard_map.50), channel_id=1, source_target_pairs={{0,16},{1,9},{2,18},{3,11},{4,20},{5,13},{6,22},{7,15},{8,24},{9,1... | collective-permute-start | bytes 1216520 | tf_op jit(solution)/shard_map/ppermute | solution.py:36
  17.3 1.5 %collective-permute-start.6 = (bf16[512,256]{1,0:T(8,128)(2,1)S(1)}, bf16[512,256]{1,0:T(8,128)(2,1)S(1)}, u32[]{:S(2)}, u32[]{:S(2)}) collective-permute-start(bf16[512,256]{1,0:T(8,128)(2,1)S(1)} %get-tuple-element.49), channel_id=1, source_target_pairs={{0,8},{1,17},{2,10},{3,19},{4,12},{5,21},{6,14},{7,23},{8,0},{9,25... | collective-permute-start | bytes 786440 | tf_op jit(solution)/shard_map/ppermute | solution.py:36
  18.8 5.5 %collective-permute-done.6.r.a = bf16[512,256]{1,0:T(8,128)(2,1)S(1)} collective-permute-done((bf16[512,256]{1,0:T(8,128)(2,1)S(1)}, bf16[512,256]{1,0:T(8,128)(2,1)S(1)}, u32[]{:S(2)}, u32[]{:S(2)}) %collective-permute-start.6) | collective-permute-done | bytes 262176 | tf_op jit(solution)/shard_map/ppermute | solution.py:36
  24.4 1.8 %collective-permute-start.7 = (bf16[512,128]{1,0:T(8,128)(2,1)S(1)}, bf16[512,128]{1,0:T(8,128)(2,1)S(1)}, u32[]{:S(2)}, u32[]{:S(2)}) collective-permute-start(bf16[512,128]{1,0:T(8,128)(2,1)S(1)} %shard_map.52), channel_id=1, source_target_pairs={{0,16},{1,9},{2,18},{3,11},{4,20},{5,13},{6,22},{7,15},{8,24},{9,1... | collective-permute-start | bytes 393224 | tf_op jit(solution)/shard_map/ppermute | solution.py:36
  26.2 1.0 %shard_map.48 = (f32[512,256]{1,0:T(8,128)S(1)}, f32[512,256]{1,0:T(8,128)S(1)}, f32[512,256]{1,0:T(8,128)S(1)}, bf16[512,256]{1,0:T(8,128)(2,1)S(1)}, bf16[512,...) custom-call(bf16[512,512]{1,0:T(8,128)(2,1)S(1)} %get-tuple-element.32.xg_ref.x, ...), custom_call_target="tpu_custom_call" | custom-call | flops 805306368 | bytes 6029312 | tf_op jit(solution)/shard_map/pallas_call | solution.py:64
  27.2 0.0 copy-start
  27.2 0.0 collective-permute-done.5.b
  27.2 0.5 %shard_map.51 = (bf16[512,256]{1,0:T(8,128)(2,1)S(1)}, bf16[512,128]{1,0:T(8,128)(2,1)S(1)}, f32[512,128]{1,0:T(8,128)S(1)}, f32[128,128]{1,0:T(8,128)S(1)}) custom-call(f32[512,256]{1,0:T(8,128)S(1)} %get-tuple-element.40.own_k, f32[512,256]{1,0:T(8,128)S(1)} %get-tuple-element.41.own_v.own, bf16[512,512]{1,0:T(8,128)(2,1)S(1)} %collective-permute-done.3.r.a, ...), custom_call_target="tpu_custom_call" | custom-call | flops 16777216 | bytes 3002368 | tf_op jit(solution)/shard_map/pallas_call | solution.py:64
  27.7 1.7 %collective-permute-done.7.b = bf16[512,128]{1,0:T(8,128)(2,1)S(1)} collective-permute-done((bf16[512,128]{1,0:T(8,128)(2,1)S(1)}, bf16[512,128]{1,0:T(8,128)(2,1)S(1)}, u32[]{:S(2)}, u32[]{:S(2)}) %collective-permute-start.7) | collective-permute-done | bytes 131104 | tf_op jit(solution)/shard_map/ppermute | solution.py:36
  29.4 0.2 shard_map.53
  29.6 0.1 collective-permute-start.8
  29.7 1.8 %collective-permute-start = (bf16[512,256]{1,0:T(8,128)(2,1)S(1)}, bf16[512,256]{1,0:T(8,128)(2,1)S(1)}, u32[]{:S(2)}, u32[]{:S(2)}) collective-permute-start(bf16[512,256]{1,0:T(8,128)(2,1)S(1)} %get-tuple-element.37), channel_id=1, source_target_pairs={{0,16},{1,9},{2,18},{3,11},{4,20},{5,13},{6,22},{7,15},{8,24},{9,1... | collective-permute-start | bytes 786440 | tf_op jit(solution)/shard_map/ppermute | solution.py:36
  31.5 1.5 %collective-permute-start.1 = (bf16[512,256]{1,0:T(8,128)(2,1)S(1)}, bf16[512,256]{1,0:T(8,128)(2,1)S(1)}, u32[]{:S(2)}, u32[]{:S(2)}) collective-permute-start(bf16[512,256]{1,0:T(8,128)(2,1)S(1)} %get-tuple-element.38), channel_id=1, source_target_pairs={{0,8},{1,17},{2,10},{3,19},{4,12},{5,21},{6,14},{7,23},{8,0},{9,25... | collective-permute-start | bytes 786440 | tf_op jit(solution)/shard_map/ppermute | solution.py:36
  33.0 0.3 collective-permute-start.2
  33.3 0.0 collective-permute-done.8.refs_1_
  33.3 1.9 %collective-permute-start.9 = (bf16[128,128]{1,0:T(8,128)(2,1)S(1)}, bf16[128,128]{1,0:T(8,128)(2,1)S(1)}, u32[]{:S(2)}, u32[]{:S(2)}) collective-permute-start(bf16[128,128]{1,0:T(8,128)(2,1)S(1)} %add_convert_fusion), channel_id=1, source_target_pairs={{0,2},{1,3},{2,0},{3,1},{4,6},{5,7},{6,4},{7,5},{8,10},{9,11},{10,... | collective-permute-start | bytes 98312 | tf_op jit(solution)/shard_map/ppermute | solution.py:26
  35.1 2.6 %collective-permute-start.10 = (bf16[128,128]{1,0:T(8,128)(2,1)S(1)}, bf16[128,128]{1,0:T(8,128)(2,1)S(1)}, u32[]{:S(2)}, u32[]{:S(2)}) collective-permute-start(bf16[128,128]{1,0:T(8,128)(2,1)S(1)} %add_convert_fusion), channel_id=1, source_target_pairs={{0,4},{1,5},{2,6},{3,7},{4,0},{5,1},{6,2},{7,3},{8,12},{9,13},{10,... | collective-permute-start | bytes 98312 | tf_op jit(solution)/shard_map/ppermute | solution.py:26
  37.7 0.0 collective-permute-done.9.refs_2_
  37.7 3.4 %collective-permute-start.11 = (bf16[128,128]{1,0:T(8,128)(2,1)S(1)}, bf16[128,128]{1,0:T(8,128)(2,1)S(1)}, u32[]{:S(2)}, u32[]{:S(2)}) collective-permute-start(bf16[128,128]{1,0:T(8,128)(2,1)S(1)} %add_convert_fusion), channel_id=1, source_target_pairs={{0,6},{1,7},{2,4},{3,5},{4,2},{5,3},{6,0},{7,1},{8,14},{9,15},{10,... | collective-permute-start | bytes 98312 | tf_op jit(solution)/shard_map/ppermute | solution.py:26
  41.1 0.0 collective-permute-done.10.refs_3_
  41.1 2.3 %collective-permute-done.11.refs_4_ = bf16[128,128]{1,0:T(8,128)(2,1)S(1)} collective-permute-done((bf16[128,128]{1,0:T(8,128)(2,1)S(1)}, bf16[128,128]{1,0:T(8,128)(2,1)S(1)}, u32[]{:S(2)}, u32[]{:S(2)}) %collective-permute-start.11) | collective-permute-done | bytes 32800 | tf_op jit(solution)/shard_map/ppermute | solution.py:26
  43.5 0.1 collective-permute-start.12
  43.6 0.0 collective-permute-done.r1
  43.6 0.0 collective-permute-done.1.r2
  43.6 1.6 %collective-permute-done.2.r3 = bf16[512,256]{1,0:T(8,128)(2,1)S(1)} collective-permute-done((bf16[512,256]{1,0:T(8,128)(2,1)S(1)}, bf16[512,256]{1,0:T(8,128)(2,1)S(1)}, u32[]{:S(2)}, u32[]{:S(2)}) %collective-permute-start.2) | collective-permute-done | bytes 262176 | tf_op jit(solution)/shard_map/ppermute | solution.py:26
  45.2 0.8 %shard_map.54 = (bf16[512,256]{1,0:T(8,128)(2,1)S(1)}, f32[512,256]{1,0:T(8,128)S(1)}) custom-call(f32[512,256]{1,0:T(8,128)S(1)} %get-tuple-element.36.own, bf16[512,256]{1,0:T(8,128)(2,1)S(1)} %collective-permute-done.r1, bf16[512,256]{1,0:T(8,128)(2,1)S(1)} %collective-permute-done.1.r2, bf16[512,256]{1,0:T(8,128)(2,1)S(1)} %collective-permute-done.2.r3, ...), custom_call_target="tpu_custom_call" | custom-call | flops 268435456 | bytes 2883584 | tf_op jit(solution)/shard_map/pallas_call | solution.py:64
  46.0 0.0 collective-permute-done.12.other
  46.1 0.0 copy-done
  46.1 1.1 %shard_map.56 = bf16[512,256]{1,0:T(8,128)(2,1)} custom-call(bf16[512,256]{1,0:T(8,128)(2,1)S(1)} %get-tuple-element.53.q, f32[512,256]{1,0:T(8,128)S(1)} %get-tuple-element.54.inner, bf16[128,128]{1,0:T(8,128)(2,1)S(1)} %get-tuple-element.57.ours, bf16[128,128]{1,0:T(8,128)(2,1)S(1)} %collective-permute-done.12.other, f32[1,256]{1,0:T(1,128)S(1)} %bitcast.2), custom_call_target="tpu_custom_call" | custom-call | flops 33554432 | bytes 1115136 | tf_op jit(solution)/shard_map/pallas_call | solution.py:64
  (3 shorter events, 0.1 us)
Async XLA Ops:
  2.0 13.1 %collective-permute-start.3 = (bf16[512,512]{1,0:T(8,128)(2,1)S(1)}, bf16[512,512]{1,0:T(8,128)(2,1)S(1)}, u32[]{:S(2)}, u32[]{:S(2)}) collective-permute-start(bf16[512,512]{1,0:T(8,128)(2,1)S(1)} %get-tuple-element.42), channel_id=1, source_target_pairs={{0,8},{1,17},{2,10},{3,19},{4,12},{5,21},{6,14},{7,23},{8,0},{9,25... | collective-permute-start | bytes 1572872 | tf_op jit(solution)/shard_map/ppermute | solution.py:36
  7.1 8.0 %collective-permute-start.4 = (bf16[528,256]{1,0:T(8,128)(2,1)S(1)}, bf16[528,256]{1,0:T(8,128)(2,1)S(1)}, u32[]{:S(2)}, u32[]{:S(2)}) collective-permute-start(bf16[528,256]{1,0:T(8,128)(2,1)S(1)} %get-tuple-element.43), channel_id=1, source_target_pairs={{0,8},{1,17},{2,10},{3,19},{4,12},{5,21},{6,14},{7,23},{8,0},{9,25... | collective-permute-start | bytes 811016 | tf_op jit(solution)/shard_map/ppermute | solution.py:36
  15.2 12.0 %collective-permute-start.5 = (bf16[528,384]{1,0:T(8,128)(2,1)S(1)}, bf16[528,384]{1,0:T(8,128)(2,1)S(1)}, u32[]{:S(2)}, u32[]{:S(2)}) collective-permute-start(bf16[528,384]{1,0:T(8,128)(2,1)S(1)} %shard_map.50), channel_id=1, source_target_pairs={{0,16},{1,9},{2,18},{3,11},{4,20},{5,13},{6,22},{7,15},{8,24},{9,1... | collective-permute-start | bytes 1216520 | tf_op jit(solution)/shard_map/ppermute | solution.py:36
  17.3 7.0 %collective-permute-start.6 = (bf16[512,256]{1,0:T(8,128)(2,1)S(1)}, bf16[512,256]{1,0:T(8,128)(2,1)S(1)}, u32[]{:S(2)}, u32[]{:S(2)}) collective-permute-start(bf16[512,256]{1,0:T(8,128)(2,1)S(1)} %get-tuple-element.49), channel_id=1, source_target_pairs={{0,8},{1,17},{2,10},{3,19},{4,12},{5,21},{6,14},{7,23},{8,0},{9,25... | collective-permute-start | bytes 786440 | tf_op jit(solution)/shard_map/ppermute | solution.py:36
  24.4 5.0 %collective-permute-start.7 = (bf16[512,128]{1,0:T(8,128)(2,1)S(1)}, bf16[512,128]{1,0:T(8,128)(2,1)S(1)}, u32[]{:S(2)}, u32[]{:S(2)}) collective-permute-start(bf16[512,128]{1,0:T(8,128)(2,1)S(1)} %shard_map.52), channel_id=1, source_target_pairs={{0,16},{1,9},{2,18},{3,11},{4,20},{5,13},{6,22},{7,15},{8,24},{9,1... | collective-permute-start | bytes 393224 | tf_op jit(solution)/shard_map/ppermute | solution.py:36
  27.2 18.9 %copy-start = (f32[256]{0:T(256)S(1)}, f32[256]{0:T(256)}, u32[]{:S(2)}) copy-start(f32[256]{0:T(256)} %param.7) | copy-start | bytes 3076
  29.6 3.6 %collective-permute-start.8 = (bf16[128,128]{1,0:T(8,128)(2,1)S(1)}, bf16[128,128]{1,0:T(8,128)(2,1)S(1)}, u32[]{:S(2)}, u32[]{:S(2)}) collective-permute-start(bf16[128,128]{1,0:T(8,128)(2,1)S(1)} %get-tuple-element.56), channel_id=1, source_target_pairs={{0,1},{1,0},{2,3},{3,2},{4,5},{5,4},{6,7},{7,6},{8,9},{9,8},{10,11... | collective-permute-start | bytes 98312 | tf_op jit(solution)/shard_map/ppermute | solution.py:26
  29.7 13.9 %collective-permute-start = (bf16[512,256]{1,0:T(8,128)(2,1)S(1)}, bf16[512,256]{1,0:T(8,128)(2,1)S(1)}, u32[]{:S(2)}, u32[]{:S(2)}) collective-permute-start(bf16[512,256]{1,0:T(8,128)(2,1)S(1)} %get-tuple-element.37), channel_id=1, source_target_pairs={{0,16},{1,9},{2,18},{3,11},{4,20},{5,13},{6,22},{7,15},{8,24},{9,1... | collective-permute-start | bytes 786440 | tf_op jit(solution)/shard_map/ppermute | solution.py:36
  31.5 12.1 %collective-permute-start.1 = (bf16[512,256]{1,0:T(8,128)(2,1)S(1)}, bf16[512,256]{1,0:T(8,128)(2,1)S(1)}, u32[]{:S(2)}, u32[]{:S(2)}) collective-permute-start(bf16[512,256]{1,0:T(8,128)(2,1)S(1)} %get-tuple-element.38), channel_id=1, source_target_pairs={{0,8},{1,17},{2,10},{3,19},{4,12},{5,21},{6,14},{7,23},{8,0},{9,25... | collective-permute-start | bytes 786440 | tf_op jit(solution)/shard_map/ppermute | solution.py:36
  33.0 12.2 %collective-permute-start.2 = (bf16[512,256]{1,0:T(8,128)(2,1)S(1)}, bf16[512,256]{1,0:T(8,128)(2,1)S(1)}, u32[]{:S(2)}, u32[]{:S(2)}) collective-permute-start(bf16[512,256]{1,0:T(8,128)(2,1)S(1)} %get-tuple-element.39), channel_id=1, source_target_pairs={{0,24},{8,16},{16,8},{24,0},{1,25},{9,17},{17,9},{25,1},{2,26},{10... | collective-permute-start | bytes 786440 | tf_op jit(solution)/shard_map/ppermute | solution.py:26
  33.3 4.5 %collective-permute-start.9 = (bf16[128,128]{1,0:T(8,128)(2,1)S(1)}, bf16[128,128]{1,0:T(8,128)(2,1)S(1)}, u32[]{:S(2)}, u32[]{:S(2)}) collective-permute-start(bf16[128,128]{1,0:T(8,128)(2,1)S(1)} %add_convert_fusion), channel_id=1, source_target_pairs={{0,2},{1,3},{2,0},{3,1},{4,6},{5,7},{6,4},{7,5},{8,10},{9,11},{10,... | collective-permute-start | bytes 98312 | tf_op jit(solution)/shard_map/ppermute | solution.py:26
  35.1 6.0 %collective-permute-start.10 = (bf16[128,128]{1,0:T(8,128)(2,1)S(1)}, bf16[128,128]{1,0:T(8,128)(2,1)S(1)}, u32[]{:S(2)}, u32[]{:S(2)}) collective-permute-start(bf16[128,128]{1,0:T(8,128)(2,1)S(1)} %add_convert_fusion), channel_id=1, source_target_pairs={{0,4},{1,5},{2,6},{3,7},{4,0},{5,1},{6,2},{7,3},{8,12},{9,13},{10,... | collective-permute-start | bytes 98312 | tf_op jit(solution)/shard_map/ppermute | solution.py:26
  37.7 5.7 %collective-permute-start.11 = (bf16[128,128]{1,0:T(8,128)(2,1)S(1)}, bf16[128,128]{1,0:T(8,128)(2,1)S(1)}, u32[]{:S(2)}, u32[]{:S(2)}) collective-permute-start(bf16[128,128]{1,0:T(8,128)(2,1)S(1)} %add_convert_fusion), channel_id=1, source_target_pairs={{0,6},{1,7},{2,4},{3,5},{4,2},{5,3},{6,0},{7,1},{8,14},{9,15},{10,... | collective-permute-start | bytes 98312 | tf_op jit(solution)/shard_map/ppermute | solution.py:26
  43.5 2.5 %collective-permute-start.12 = (bf16[128,128]{1,0:T(8,128)(2,1)S(1)}, bf16[128,128]{1,0:T(8,128)(2,1)S(1)}, u32[]{:S(2)}, u32[]{:S(2)}) collective-permute-start(bf16[128,128]{1,0:T(8,128)(2,1)S(1)} %get-tuple-element.58), channel_id=1, source_target_pairs={{0,1},{1,0},{2,3},{3,2},{4,5},{5,4},{6,7},{7,6},{8,9},{9,8},{10,11... | collective-permute-start | bytes 98312 | tf_op jit(solution)/shard_map/ppermute | solution.py:26
